TPU v7x, 32 devices: a whole 2x2x4 slice. The times are simulated.
32 devices in a mesh: ctx: 8 (over z, x), fsdp: 4 (over y, core).
Axes of the slice: x: 2, y: 2, z: 4, core: 2. Of those that a mesh axis runs over, the one named last changes fastest.
Arguments:
- inputs: bfloat16 [4, 4096, 768], P('fsdp', 'ctx'), may hold values from -6 to 6
- doc_starts: int32 [4, 8], P('fsdp'), may hold values from 0 to 4095, as said below
- qkv_weight: bfloat16 [768, 2304], P('fsdp'), may hold values from -0.21875 to 0.21875
- query_bias: bfloat16 [768], P('fsdp'), may hold values from -3 to 3
- value_bias: bfloat16 [768], P('fsdp'), may hold values from -3 to 3
- out_weight: bfloat16 [768, 768], P('fsdp'), may hold values from -2 to 2
- out_bias: bfloat16 [768], P('fsdp'), may hold values from -2 to 2
- norm1_gain: bfloat16 [768], P('fsdp'), may hold values from 0.25 to 1.75
- norm1_bias: bfloat16 [768], P('fsdp'), may hold values from -2 to 2
- in_weight: bfloat16 [768, 3072], P('fsdp'), may hold values from -0.21875 to 0.21875
- in_bias: bfloat16 [3072], P('fsdp'), may hold values from -3 to 3
- back_weight: bfloat16 [3072, 768], P('fsdp'), may hold values from -0.109375 to 0.109375
- back_bias: bfloat16 [768], P('fsdp'), may hold values from -2 to 2
- norm2_gain: bfloat16 [768], P('fsdp'), may hold values from 0.25 to 1.75
- norm2_bias: bfloat16 [768], P('fsdp'), may hold values from -2 to 2
- cotangent: bfloat16 [4, 4096, 768], P('fsdp', 'ctx'), may hold values from -6 to 6
Outputs:
- output: bfloat16 [4, 4096, 768], P('fsdp', 'ctx')
- input_grad: float32 [4, 4096, 768], P('fsdp', 'ctx')
- qkv_weight_grad: float32 [768, 2304], P('fsdp')
- query_bias_grad: float32 [768], P('fsdp')
- value_bias_grad: float32 [768], P('fsdp')
- out_weight_grad: float32 [768, 768], P('fsdp')
- out_bias_grad: float32 [768], P('fsdp')
- norm1_gain_grad: float32 [768], P('fsdp')
- norm1_bias_grad: float32 [768], P('fsdp')
- in_weight_grad: float32 [768, 3072], P('fsdp')
- in_bias_grad: float32 [3072], P('fsdp')
- back_weight_grad: float32 [3072, 768], P('fsdp')
- back_bias_grad: float32 [768], P('fsdp')
- norm2_gain_grad: float32 [768], P('fsdp')
- norm2_bias_grad: float32 [768], P('fsdp')
Inputs may be any that keep to these rules, and one draw needn't show every extreme that they name: `doc_starts`: row s lists the first positions of the 8 documents of stream s in increasing order, all different; the first is 0 and the last is 4095, a one-token document at the stream's end. A document runs from its start to the next start.
All inputs are finite; a program needn't handle non-finite values.
Results may differ from a plain program's by a relative error of at most 0.022.
Values may be sent and summed in bfloat16 or wider, within the bound.
No kernel may reach another device: no remote copies, remote signals or barrier semaphores. Data moves between devices by JAX's collectives and lax.ppermute only.
A program may use at most 192 MiB of HBM per device.

v0:
```python
from functools import partial
import math

import jax
import jax.numpy as jnp
from jax import lax
from jax.experimental import pallas as pl
from jax.experimental.pallas import tpu as pltpu
from jax.sharding import PartitionSpec as P

H = 12
HD = 64
EPSILON = 1e-05
BIG = 2.0**100
LOG2E = 1.4426950408889634
PAD = 16
KERNEL_FLOPS = 3_000_000_000
KERNEL_BYTES = 20_000_000


def ctx_swap(array, groups, parts, flip):
    pairs = []
    for g in range(groups):
        for s in range(parts):
            pairs.append((g * parts + s, (g ^ flip) * parts + s))
    return lax.ppermute(array, "ctx", pairs)


def part_shift(array, groups, parts, by):
    pairs = []
    for g in range(groups):
        for s in range(parts):
            pairs.append((g * parts + s, g * parts + (s + by) % parts))
    return lax.ppermute(array, "ctx", pairs)


def gather_groups(array, groups, parts):
    return [array] + [ctx_swap(array, groups, parts, i) for i in range(1, groups)]


def swap(array, axis, bit):
    size = lax.axis_size(axis)
    return lax.ppermute(array, axis, [(i, i ^ (1 << bit)) for i in range(size)])


def bits_of(axis):
    return lax.axis_size(axis).bit_length() - 1


def bit_at(axis, bit):
    return (lax.axis_index(axis) >> bit) & 1


def pick(array, which, dim):
    return lax.dynamic_index_in_dim(array, which, dim, keepdims=False)


def together(*values):
    return lax.optimization_barrier(values)


def join(mine, own, other, dim):
    return jnp.where(
        mine == 0,
        jnp.concatenate([own, other], axis=dim),
        jnp.concatenate([other, own], axis=dim),
    )


def gather_top(shard):
    return swap(shard, "fsdp", bits_of("fsdp") - 1)


def gather_rest(shard, other):
    top = bits_of("fsdp") - 1
    held = join(bit_at("fsdp", top), shard[None], other[None], 0)
    for bit in reversed(range(top)):
        got = swap(held, "fsdp", bit)
        pair = join(bit_at("fsdp", bit), held[:, None], got[:, None], 1)
        held = pair.reshape((-1,) + shard.shape)
    return held


def halve(held, axis, bit, dim):
    mine = bit_at(axis, bit)
    if axis == "fsdp":
        pairs = held.reshape((held.shape[0] // 2, 2) + held.shape[1:])
        keep, send = pick(pairs, mine, 1), pick(pairs, 1 - mine, 1)
    else:
        half = held.shape[dim] // 2
        keep = lax.dynamic_slice_in_dim(held, mine * half, half, dim)
        send = lax.dynamic_slice_in_dim(held, (1 - mine) * half, half, dim)
    return add_low(keep, swap(send, axis, bit))


def add_low(a, b):
    return (a.astype(jnp.float32) + b.astype(jnp.float32)).astype(jnp.bfloat16)


def double(held, axis, bit, dim):
    return join(bit_at(axis, bit), held, swap(held, axis, bit), dim)


def doc_row(meta, base, length, docs):
    pos = base + lax.broadcasted_iota(jnp.int32, (1, length), 1)
    doc = jnp.full((1, length), -1, jnp.int32)
    for j in range(docs):
        doc = doc + (pos >= meta[2 + j]).astype(jnp.int32)
    return doc


def dot(a, b):
    return jnp.dot(a, b, preferred_element_type=jnp.float32)


def dot_t(a, b):
    return lax.dot_general(a, b, (((1,), (1,)), ((), ())), preferred_element_type=jnp.float32)


def fill_keys(meta, own, others, groups, parts, docs, rows, store):
    g, s = meta[0], meta[1]
    for j in range(groups):
        for e in range(parts):
            block = (g ^ j) * parts + lax.rem(s - e + parts, parts)
            if e == 0:
                key_t, value_t = own[j][1, 0], own[j][2, 0]
            else:
                ref = others[(e - 1) * groups + j]
                key_t, value_t = ref[0, 0], ref[1, 0]
            doc = doc_row(meta, block * rows, rows, docs)
            hot = (lax.broadcasted_iota(jnp.int32, (HD, rows), 0) == doc).astype(jnp.float32)
            keys = jnp.concatenate([key_t, hot.astype(jnp.bfloat16)], axis=0)
            store(block, keys, key_t, value_t)


def query_full(meta, query_t, j, groups, parts, docs, rows):
    g, s = meta[0], meta[1]
    block = (g ^ j) * parts + s
    doc = doc_row(meta, block * rows, rows, docs)
    shut = jnp.where(lax.broadcasted_iota(jnp.int32, (HD, rows), 0) == doc, 0.0, -BIG)
    return jnp.concatenate([query_t, shut.astype(jnp.bfloat16)], axis=0)


def attend_kernel(groups, parts, docs, rows, meta, *refs):
    own = refs[:groups]
    others = refs[groups : groups * parts]
    low_ref, wide_ref, log_ref, queries_ref, keys_ref, values_ref = refs[groups * parts :]
    coeff = LOG2E * HD**-0.5

    def store(block, keys, key_t, value_t):
        keys_ref[block] = keys.T
        values_ref[block] = value_t

    fill_keys(meta, own, others, groups, parts, docs, rows, store)
    for j in range(groups):
        queries_ref[j] = query_full(meta, own[j][0, 0], j, groups, parts, docs, rows)

    def one_slot(j, carry):
        full = queries_ref[j]

        def step(t, state):
            best, total, accum = state
            scores = dot(keys_ref[t], full)
            new_best = jnp.maximum(best, jnp.max(scores, axis=0, keepdims=True))
            weights = jnp.exp2((scores - new_best) * coeff)
            shrink = jnp.exp2((best - new_best) * coeff)
            total = total * shrink + jnp.sum(weights, axis=0, keepdims=True)
            accum = accum * shrink + dot(values_ref[t], weights.astype(jnp.bfloat16))
            return new_best, total, accum

        best, total, accum = lax.fori_loop(
            meta[2 + docs + 2 * j],
            meta[3 + docs + 2 * j],
            step,
            (
                jnp.full((1, rows), -BIG, jnp.float32),
                jnp.zeros((1, rows), jnp.float32),
                jnp.zeros((HD, rows), jnp.float32),
            ),
        )
        attended = accum / total
        at = pl.ds(pl.multiple_of(j * rows, rows), rows)
        wide_ref[0, :, at] = attended
        low_ref[0, :, at] = attended.astype(jnp.bfloat16)
        log_ref[0, :, at] = best * coeff + jnp.log2(total)
        return carry

    lax.fori_loop(0, groups, one_slot, 0)


def attend_back_kernel(groups, parts, docs, rows, meta, *refs):
    own = refs[:groups]
    others = refs[groups : groups * parts]
    grads = refs[groups * parts : groups * parts + groups]
    rest = refs[groups * parts + groups :]
    wide_ref, log_ref = rest[:2]
    dq_ref, mine_ref = rest[2:4]
    theirs = rest[4] if parts > 1 else None
    queries_ref, grads_ref, keys_ref, keys_t_ref, values_ref, accum_ref = rest[-6:]
    coeff = LOG2E * HD**-0.5

    def store(block, keys, key_t, value_t):
        keys_ref[block] = keys.T
        keys_t_ref[block] = key_t
        values_ref[block] = value_t.T

    fill_keys(meta, own, others, groups, parts, docs, rows, store)
    accum_ref[...] = jnp.zeros_like(accum_ref)
    for j in range(groups):
        queries_ref[j] = query_full(meta, own[j][0, 0], j, groups, parts, docs, rows)
        grads_ref[j] = grads[j][0]

    def one_slot(j, carry):
        at = pl.ds(pl.multiple_of(j * rows, rows), rows)
        full = queries_ref[j]
        grad_t = grads_ref[j]
        delta = jnp.sum(grad_t.astype(jnp.float32) * wide_ref[0, :, at], axis=0, keepdims=True)
        log_total = log_ref[0, :, at]
        blank = jnp.zeros((HD, rows), jnp.bfloat16)
        both = jnp.concatenate(
            [
                jnp.concatenate([full[:HD], blank], axis=1),
                jnp.concatenate([blank, grad_t], axis=1),
            ],
            axis=0,
        )

        def step(t, grad_query):
            scores = dot(keys_ref[t], full)
            probs = jnp.exp2(scores * coeff - log_total)
            d_probs = dot(values_ref[t], grad_t)
            d_scores = (probs * (d_probs - delta)).astype(jnp.bfloat16)
            joined = jnp.concatenate([d_scores, probs.astype(jnp.bfloat16)], axis=1)
            accum_ref[t] += dot_t(joined, both)
            return grad_query + dot(keys_t_ref[t], d_scores)

        grad_query = lax.fori_loop(
            meta[2 + docs + 2 * j],
            meta[3 + docs + 2 * j],
            step,
            jnp.zeros((HD, rows), jnp.float32),
        )
        dq_ref[:, at] = (grad_query * HD**-0.5).astype(jnp.bfloat16)
        return carry

    lax.fori_loop(0, groups, one_slot, 0)
    g, s = meta[0], meta[1]
    for j in range(groups):
        for e in range(parts):
            block = (g ^ j) * parts + lax.rem(s - e + parts, parts)
            terms = accum_ref[block].T
            at = slice(j * rows, (j + 1) * rows)
            d_key = terms[:HD] * HD**-0.5
            d_value = terms[HD:]
            if e == 0:
                mine_ref[0, :, at] = d_key
                mine_ref[1, :, at] = d_value
            else:
                theirs[e - 1, 0, :, at] = d_key.astype(jnp.bfloat16)
                theirs[e - 1, 1, :, at] = d_value.astype(jnp.bfloat16)


def head_block(head, *shape):
    dims = tuple(1 if n is None else n for n in shape)
    where = shape.index(None)

    def at(h, meta):
        chosen = h if head is None else head
        return tuple(chosen if i == where else 0 for i in range(len(dims)))

    return pl.BlockSpec(dims, at)


def attend(meta, own, others, groups, parts, docs, rows, heads):
    tiles = groups * parts
    tokens = groups * rows
    block = partial(head_block, None)
    grid_spec = pltpu.PrefetchScalarGridSpec(
        num_scalar_prefetch=1,
        grid=(heads,),
        in_specs=[block(3, None, HD, rows)] * groups
        + [block(2, None, HD, rows)] * (groups * (parts - 1)),
        out_specs=[block(None, HD, tokens), block(None, HD, tokens), block(None, 1, tokens)],
        scratch_shapes=[
            pltpu.VMEM((groups, 2 * HD, rows), jnp.bfloat16),
            pltpu.VMEM((tiles, rows, 2 * HD), jnp.bfloat16),
            pltpu.VMEM((tiles, HD, rows), jnp.bfloat16),
        ],
    )
    return pl.pallas_call(
        partial(attend_kernel, groups, parts, docs, rows),
        grid_spec=grid_spec,
        out_shape=[
            jax.ShapeDtypeStruct((heads, HD, tokens), jnp.bfloat16),
            jax.ShapeDtypeStruct((heads, HD, tokens), jnp.float32),
            jax.ShapeDtypeStruct((heads, 1, tokens), jnp.float32),
        ],
        cost_estimate=pl.CostEstimate(
            flops=KERNEL_FLOPS * 2 * heads,
            transcendentals=0,
            bytes_accessed=KERNEL_BYTES * heads,
        ),
        name="attend",
    )(meta, *own, *others)


def attend_back(head, meta, own, others, grads, wide, log_total, groups, parts, docs, rows):
    tiles = groups * parts
    tokens = groups * rows
    block = partial(head_block, head)
    plain = lambda *dims: pl.BlockSpec(dims, lambda h, meta: (0,) * len(dims))
    out_specs = [plain(HD, tokens), plain(2, HD, tokens)]
    out_shape = [
        jax.ShapeDtypeStruct((HD, tokens), jnp.bfloat16),
        jax.ShapeDtypeStruct((2, HD, tokens), jnp.float32),
    ]
    if parts > 1:
        out_specs.append(plain(parts - 1, 2, HD, tokens))
        out_shape.append(jax.ShapeDtypeStruct((parts - 1, 2, HD, tokens), jnp.bfloat16))
    grid_spec = pltpu.PrefetchScalarGridSpec(
        num_scalar_prefetch=1,
        grid=(1,),
        in_specs=[block(3, None, HD, rows)] * groups
        + [block(2, None, HD, rows)] * (groups * (parts - 1))
        + [block(None, HD, rows)] * groups
        + [block(None, HD, tokens), block(None, 1, tokens)],
        out_specs=out_specs,
        scratch_shapes=[
            pltpu.VMEM((groups, 2 * HD, rows), jnp.bfloat16),
            pltpu.VMEM((groups, HD, rows), jnp.bfloat16),
            pltpu.VMEM((tiles, rows, 2 * HD), jnp.bfloat16),
            pltpu.VMEM((tiles, HD, rows), jnp.bfloat16),
            pltpu.VMEM((tiles, rows, HD), jnp.bfloat16),
            pltpu.VMEM((tiles, rows, 2 * HD), jnp.float32),
        ],
    )
    return pl.pallas_call(
        partial(attend_back_kernel, groups, parts, docs, rows),
        grid_spec=grid_spec,
        out_shape=out_shape,
        cost_estimate=pl.CostEstimate(
            flops=KERNEL_FLOPS * 5, transcendentals=0, bytes_accessed=KERNEL_BYTES
        ),
        name="attend_back",
    )(meta, *own, *others, *grads, wide, log_total)


ERFC = (
    -1.26551223, 1.00002368, 0.37409196, 0.09678418, -0.18628806,
    0.27886807, -1.13520398, 1.48851587, -0.82215223, 0.17087277,
)


def normal_terms(v):
    z = jnp.abs(v) * (0.5**0.5)
    t = 1.0 / (1.0 + 0.5 * z)
    poly = jnp.full_like(t, ERFC[-1])
    for term in reversed(ERFC[:-1]):
        poly = poly * t + term
    square = z * z
    tail = 0.5 * t * jnp.exp(poly - square)
    below = jnp.where(v < 0, tail, 1.0 - tail)
    return below, jnp.exp(-square) * (2.0 * math.pi) ** -0.5


def normed(resid):
    centred = resid - jnp.mean(resid, axis=-1, keepdims=True)
    spread = jnp.mean(centred * centred, axis=-1, keepdims=True)
    scale = lax.rsqrt(spread + EPSILON)
    return centred * scale, scale


def norm_back(grad, gain, unit, scale):
    e = grad * gain
    inner = jnp.mean(e * unit, axis=-1, keepdims=True)
    return (e - jnp.mean(e, axis=-1, keepdims=True) - unit * inner) * scale


def over_blocks(count, aligned, step, value):
    if aligned:
        return lax.fori_loop(0, count, step, value)
    for i in range(count):
        value = step(i, value)
    return value


def feed_kernel(
    tokens_ref,
    attended_ref,
    cot_ref,
    out_ref,
    in_ref,
    back_ref,
    vec_ref,
    in_bias_ref,
    result_ref,
    d_resid1_ref,
    d_attended_ref,
    hidden_ref,
    act_ref,
    d_ffn_ref,
    d_pre_ref,
    d_branch_ref,
    sums_ref,
    in_sums_ref,
    slope_ref,
):
    f32, bf16 = jnp.float32, jnp.bfloat16
    out_shift, gain_one, shift_one = vec_ref[2:3], vec_ref[3:4], vec_ref[4:5]
    back_shift, gain_two, shift_two = vec_ref[5:6], vec_ref[6:7], vec_ref[7:8]

    @pl.when(pl.program_id(0) == 0)
    def _():
        sums_ref[...] = jnp.zeros_like(sums_ref)
        in_sums_ref[...] = jnp.zeros_like(in_sums_ref)

    total = lambda a: jnp.sum(a, axis=0, keepdims=True)
    branch = dot(attended_ref[...].T, out_ref[...]) + out_shift
    unit1, scale1 = normed(tokens_ref[...].astype(f32) + branch)
    hidden = unit1 * gain_one + shift_one
    hidden_low = hidden.astype(bf16)
    count, unused, shard = hidden_ref.shape
    for i in range(count):
        hidden_ref[i] = hidden_low[:, i * shard : (i + 1) * shard]
    resid2 = hidden + back_shift
    blocks, unused, size = act_ref.shape
    aligned = size % 128 == 0
    columns = lambda i: pl.ds(pl.multiple_of(i * size, size) if aligned else i * size, size)

    def forward(i, resid2):
        cols = columns(i)
        pre = dot(hidden_low, in_ref[:, cols]) + in_bias_ref[:, cols]
        below, density = normal_terms(pre)
        act = (pre * below).astype(bf16)
        act_ref[i] = act
        slope_ref[i] = below + pre * density
        return resid2 + dot(act, back_ref[cols, :])

    resid2 = over_blocks(blocks, aligned, forward, hidden + back_shift)
    unit2, scale2 = normed(resid2)
    result_ref[...] = (unit2 * gain_two + shift_two).astype(bf16)
    cot = cot_ref[...].astype(f32)
    d_resid2 = norm_back(cot, gain_two, unit2, scale2)
    d_ffn = d_resid2.astype(bf16)
    d_ffn_ref[...] = d_ffn

    def backward(i, d_hidden):
        cols = columns(i)
        d_act = dot_t(d_ffn, back_ref[cols, :])
        d_pre = (d_act * slope_ref[i]).astype(bf16)
        d_pre_ref[:, cols] = d_pre
        in_sums_ref[:, cols] += total(d_pre.astype(f32))
        return d_hidden + dot_t(d_pre, in_ref[:, cols])

    d_hidden = over_blocks(blocks, aligned, backward, d_resid2)
    d_resid1 = norm_back(d_hidden, gain_one, unit1, scale1)
    d_resid1_ref[...] = d_resid1
    d_branch = d_resid1.astype(bf16)
    d_branch_ref[...] = d_branch
    d_attended_ref[...] = dot_t(out_ref[...], d_branch).astype(bf16)
    sums_ref[...] += jnp.concatenate(
        [
            total(d_branch.astype(f32)),
            total(d_hidden * unit1),
            total(d_hidden),
            total(d_ffn.astype(f32)),
            total(cot * unit2),
            total(cot),
            jnp.zeros((2, cot.shape[1]), f32),
        ],
        axis=0,
    )


def feed_forward(fsdp, tokens, attended_t, cotangent, out_full, in_full, back_full, vectors, in_shift):
    f32, bf16 = jnp.float32, jnp.bfloat16
    rows, model = tokens.shape
    inner = in_full.shape[1]
    tile = math.gcd(rows, 256)
    by_rows = lambda n: pl.BlockSpec((tile, n), lambda i: (i, 0))
    by_cols = lambda n: pl.BlockSpec((n, tile), lambda i: (0, i))
    blocks = lambda n: pl.BlockSpec((fsdp, tile, n // fsdp), lambda i: (0, i, 0))
    fixed = lambda m, n: pl.BlockSpec((m, n), lambda i: (0, 0))
    shape = jax.ShapeDtypeStruct
    return pl.pallas_call(
        feed_kernel,
        grid=(rows // tile,),
        in_specs=[
            by_rows(model), by_cols(model), by_rows(model), fixed(model, model),
            fixed(model, inner), fixed(inner, model), fixed(8, model), fixed(1, inner),
        ],
        out_specs=[
            by_rows(model), by_rows(model), by_cols(model), blocks(model), blocks(inner),
            by_rows(model), by_rows(inner), by_rows(model), fixed(8, model), fixed(1, inner),
        ],
        out_shape=[
            shape((rows, model), bf16), shape((rows, model), f32), shape((model, rows), bf16),
            shape((fsdp, rows, model // fsdp), bf16), shape((fsdp, rows, inner // fsdp), bf16),
            shape((rows, model), bf16),
            shape((rows, inner), bf16), shape((rows, model), bf16), shape((8, model), f32),
            shape((1, inner), f32),
        ],
        scratch_shapes=[pltpu.VMEM((fsdp, tile, inner // fsdp), f32)],
        cost_estimate=pl.CostEstimate(
            flops=rows * model * (8 * inner + 4 * model), transcendentals=0, bytes_accessed=30_000_000
        ),
        name="feed_forward",
    )(tokens, attended_t, cotangent, out_full, in_full, back_full, vectors, in_shift)


def weight_grad_kernel(which, *refs):
    ins, (d_ffn, d_pre, d_branch), outs = refs[:8], refs[8:11], refs[11:]
    bf16 = jnp.bfloat16
    for side in range(2):
        act, hidden, attended_t, line = ins[4 * side : 4 * side + 4]
        lower, upper = outs[2 * side : 2 * side + 2]
        first, second = act.shape[2], attended_t.shape[0]
        lower[0, :first] = dot(act[0].T, d_ffn[...]).astype(bf16)
        lower[0, first : first + second] = dot(attended_t[...], d_branch[...]).astype(bf16)
        lower[0, first + second :] = line[0].astype(bf16)
        upper[0] = dot(hidden[0].T, d_pre[...]).astype(bf16)


def weight_grads(which, act, hidden, attended_t, line, d_ffn, d_pre, d_branch):
    fsdp, rows, inner_shard = act.shape
    shard = hidden.shape[2]
    model, inner = d_ffn.shape[1], d_pre.shape[1]
    line_rows = line.shape[1]
    tall = inner_shard + shard + line_rows
    half = fsdp // 2
    in_specs = []
    for side in range(2):
        block = lambda i, w, side=side: 2 * i + w[side]
        in_specs += [
            pl.BlockSpec((1, rows, inner_shard), lambda i, w, b=block: (b(i, w), 0, 0)),
            pl.BlockSpec((1, rows, shard), lambda i, w, b=block: (b(i, w), 0, 0)),
            pl.BlockSpec((shard, rows), lambda i, w, b=block: (b(i, w), 0)),
            pl.BlockSpec((1, line_rows, model), lambda i, w, b=block: (b(i, w), 0, 0)),
        ]
    in_specs += [pl.BlockSpec((rows, n), lambda i, w: (0, 0)) for n in (model, inner, model)]
    out = [(tall, model), (shard, inner)] * 2
    return pl.pallas_call(
        weight_grad_kernel,
        grid_spec=pltpu.PrefetchScalarGridSpec(
            num_scalar_prefetch=1,
            grid=(half,),
            in_specs=in_specs,
            out_specs=[pl.BlockSpec((1,) + o, lambda i, w: (i, 0, 0)) for o in out],
        ),
        out_shape=[jax.ShapeDtypeStruct((half,) + o, jnp.bfloat16) for o in out],
        cost_estimate=pl.CostEstimate(
            flops=2 * rows * model * (2 * inner + model), transcendentals=0, bytes_accessed=25_000_000
        ),
        name="weight_grads",
    )(which, act, hidden, attended_t, line, act, hidden, attended_t, line, d_ffn, d_pre, d_branch)


def qkv_grad_kernel(fsdp, which, *refs):
    slots, (d_qkv, send, keep, total) = refs[:-4], refs[-4:]
    rows = slots[0].shape[0]
    shard = send.shape[1] - PAD
    value = None
    for j, slot in enumerate(slots):
        term = dot_t(slot[...].T, d_qkv[:, j * rows : (j + 1) * rows])
        value = term if value is None else value + term
    total[...] = value
    ones = jnp.ones((PAD, d_qkv.shape[1]), jnp.bfloat16)
    sums = dot_t(ones, d_qkv[...]).astype(jnp.bfloat16)
    for side, ref in enumerate((send, keep)):
        for i in range(fsdp // 2):
            at = pl.multiple_of((2 * i + which[side]) * shard, math.gcd(shard, 64))
            ref[i, :shard] = total[pl.ds(at, shard), :].astype(jnp.bfloat16)
            ref[i, shard:] = sums


def qkv_grads(which, slots, d_qkv_t, fsdp):
    rows, model = slots[0].shape
    width = d_qkv_t.shape[0]
    out = (fsdp // 2, model // fsdp + PAD, width)
    fixed = lambda dims: pl.BlockSpec(dims, lambda i, w: (0,) * len(dims))
    return pl.pallas_call(
        partial(qkv_grad_kernel, fsdp),
        grid_spec=pltpu.PrefetchScalarGridSpec(
            num_scalar_prefetch=1,
            grid=(1,),
            in_specs=[fixed((rows, model))] * len(slots) + [fixed(d_qkv_t.shape)],
            out_specs=[fixed(out)] * 2,
            scratch_shapes=[pltpu.VMEM((model, width), jnp.float32)],
        ),
        out_shape=[jax.ShapeDtypeStruct(out, jnp.bfloat16)] * 2,
        cost_estimate=pl.CostEstimate(
            flops=2 * rows * len(slots) * model * width, transcendentals=0, bytes_accessed=8_000_000
        ),
        name="qkv_grads",
    )(which, *slots, d_qkv_t)


def body(
    inputs,
    doc_starts,
    qkv_weight,
    query_bias,
    value_bias,
    out_weight,
    out_bias,
    norm1_gain,
    norm1_bias,
    in_weight,
    in_bias,
    back_weight,
    back_bias,
    norm2_gain,
    norm2_bias,
    cotangent,
):
    bf16, f32 = jnp.bfloat16, jnp.float32
    tokens = inputs[0]
    rows, model = tokens.shape
    starts = doc_starts[0]
    docs = starts.shape[0]
    ctx = lax.axis_size("ctx")
    fsdp = lax.axis_size("fsdp")
    groups = math.gcd(H, ctx)
    parts = ctx // groups
    heads = H // groups
    span = heads * HD
    width = 3 * span
    index = lax.axis_index("ctx")
    g, s = index // parts, index % parts
    f = lax.axis_index("fsdp")
    shard = model // fsdp

    slots = gather_groups(tokens, groups, parts)

    own_cols = pick(qkv_weight.reshape(shard, 3, groups, span), g, 2).reshape(shard, width)
    small = jnp.concatenate(
        [
            query_bias, value_bias, out_bias, norm1_gain, norm1_bias,
            back_bias, norm2_gain, norm2_bias, in_bias,
        ]
    )
    count = small.shape[0]
    extra = -(-count // (width * PAD)) * PAD
    small_block = jnp.pad(small, (0, extra * width - count)).reshape(extra, width)
    first = jnp.concatenate([own_cols, small_block], axis=0)
    first_top = gather_top(first)
    first_top, out_held, in_held, back_held = together(
        first_top, out_weight, in_weight, back_weight
    )
    out_top, in_top, back_top = gather_top(out_held), gather_top(in_held), gather_top(back_held)
    first = gather_rest(first, first_top)
    own_weight = first[:, :shard].reshape(model, width)
    flat = first[:, shard:].reshape(fsdp, extra * width)[:, :count].astype(f32)
    vectors = flat[:, : 8 * shard].reshape(fsdp, 8, shard).transpose(1, 0, 2).reshape(8, model)
    query_shift, value_shift = vectors[0], vectors[1]
    in_shift = flat[:, 8 * shard :].reshape(1, -1)

    zero = jnp.zeros((span,), f32)
    own_shift = jnp.concatenate(
        [
            lax.dynamic_slice(query_shift, (g * span,), (span,)),
            zero,
            lax.dynamic_slice(value_shift, (g * span,), (span,)),
        ]
    )
    own, others = [], []
    for slot in slots:
        projected = lax.dot_general(
            own_weight, slot, (((0,), (1,)), ((), ())), preferred_element_type=f32
        )
        low = (projected + own_shift[:, None]).astype(bf16).reshape(3, heads, HD, rows)
        own.append(low)
    for e in range(1, parts):
        for low in own:
            others.append(part_shift(low[1:], groups, parts, e))
    if parts > 1:
        in_top, others[0] = together(in_top, others[0])

    bounds = jnp.concatenate([starts, jnp.full((1,), ctx * rows, jnp.int32)])
    base = (g ^ jnp.arange(groups, dtype=jnp.int32)) * parts + s
    heads_at = base * rows
    tails_at = heads_at + rows - 1
    low_edge = jnp.max(jnp.where(starts[None] <= heads_at[:, None], starts[None], 0), axis=1)
    high_edge = jnp.min(
        jnp.where(bounds[None] > tails_at[:, None], bounds[None], ctx * rows), axis=1
    )
    ranges = jnp.stack([low_edge // rows, (high_edge + rows - 1) // rows], axis=1).reshape(-1)
    meta = jnp.concatenate([jnp.stack([g, s]).astype(jnp.int32), starts, ranges.astype(jnp.int32)])

    out_full = gather_rest(out_weight, out_top).reshape(model, model)
    in_full = gather_rest(in_weight, in_top).reshape(model, -1)
    meta, out_full, in_full = together(meta, out_full, in_full)
    low, wide, log_total = attend(meta, own, others, groups, parts, docs, rows, heads)
    attended_t = jnp.zeros((groups * span, rows), bf16)
    turned = []
    for j in range(groups):
        piece = low[:, :, j * rows : (j + 1) * rows]
        turned.append(ctx_swap(piece, groups, parts, j) if j else piece)
    for j, piece in enumerate(together(*turned)):
        attended_t = lax.dynamic_update_slice(
            attended_t, piece.reshape(span, rows), ((g ^ j) * span, 0)
        )
    back_full = gather_rest(back_weight, back_top).reshape(-1, model)

    (
        result, d_resid1, d_attended_t, hidden_low, act_low, d_ffn_low, d_pre_low, d_branch_low,
        sums, in_sums,
    ) = feed_forward(
        fsdp, tokens, attended_t, cotangent[0], out_full, in_full, back_full, vectors, in_shift
    )
    grads = []
    for j in range(groups):
        part = lax.dynamic_slice(d_attended_t, ((g ^ j) * span, 0), (span, rows))
        part = part.reshape(heads, HD, rows)
        grads.append(ctx_swap(part, groups, parts, j) if j else part)

    inner = in_full.shape[1]
    inner_shard = in_bias.shape[0]
    line = jnp.concatenate(
        [sums[:6].reshape(6, fsdp, shard).transpose(1, 0, 2).reshape(fsdp, -1), in_sums.reshape(fsdp, -1)],
        axis=1,
    )
    line_rows = -(inner_shard + shard) % 64 or 64
    line = jnp.pad(line, ((0, 0), (0, line_rows * model - line.shape[1])))
    line = line.reshape(fsdp, line_rows, model)
    mine = bit_at("fsdp", 0)
    which = jnp.stack([1 - mine, mine]).astype(jnp.int32)
    lower_send, upper_send, lower, upper = weight_grads(
        which, act_low, hidden_low, attended_t, line, d_ffn_low, d_pre_low, d_branch_low
    )
    lower = add_low(lower, swap(lower_send, "fsdp", 0))
    upper = add_low(upper, swap(upper_send, "fsdp", 0))
    fsdp_bits, ctx_bits = range(bits_of("fsdp")), range(bits_of("ctx"))
    chunks = inner // (2 * model)

    def pair_step(i, state):
        lower, upper = state
        lower_steps = [("fsdp", b) for b in fsdp_bits[1:]] + [("ctx", 0)]
        upper_steps = [("ctx", 0)] + [("fsdp", b) for b in fsdp_bits[1:]]
        return halve(lower, *lower_steps[i], 1), halve(upper, *upper_steps[i], 2)

    def merge(state):
        lower, upper = state
        return (
            jnp.concatenate(
                [lower[0]] + [upper[0, :, c * model : (c + 1) * model] for c in range(chunks)], axis=0
            ),
        )

    steps = [partial(pair_step, i) for i in range(len(fsdp_bits))]
    last = steps.pop()
    steps.append(lambda state: merge(last(state)))
    for bit in ctx_bits[1:-1]:
        steps.append(lambda state, bit=bit: (halve(state[0], "ctx", bit, 0),))
    state = (lower, upper)

    pieces = []
    held, theirs = None, None

    def settle(dq, dkv, theirs):
        for other in theirs:
            dkv = dkv + other.astype(f32)
        pieces.append(jnp.concatenate([dq[None], dkv.astype(bf16)], axis=0))

    def send(piece):
        parts_of = []
        for j in range(groups):
            part = piece[..., j * rows : (j + 1) * rows]
            parts_of.append(ctx_swap(part, groups, parts, j) if j else part)
        return parts_of

    for head in range(heads):
        meta, *state = together(meta, *state)
        flying = steps.pop(0)(state) if steps else state
        dq, dkv, *rest = attend_back(
            head, meta, own, others, grads, wide, log_total, groups, parts, docs, rows
        )
        if head:
            dq, dkv, *landed = together(dq, dkv, *rest, *flying)
            rest, state = landed[: len(rest)], landed[len(rest) :]
            dq, *theirs = together(dq, *theirs)
            settle(*held, theirs)
        else:
            state = flying
        if head == 1:
            early = send(pieces[0])
            dq, qkv_held = together(dq, qkv_weight)
            qkv_top = gather_top(qkv_held)
        elif head == 2:
            middle = send(pieces[1])
            dq, qkv_top, *early = together(dq, qkv_top, *early)
        held = (dq, dkv)
        theirs = [part_shift(rest[0][e - 1], groups, parts, -e) for e in range(1, parts)]
    settle(*held, theirs)
    for advance in steps:
        state = advance(state)
    other = swap(state[0], "ctx", ctx_bits[-1])
    count = len(middle)
    other, *landed = together(other, *middle, *pieces)
    middle, pieces = landed[:count], landed[count:]
    merged = add_low(state[0], other)
    late, merged = together(pieces[2], merged)
    for bit in reversed(ctx_bits[1:-1]):
        merged = double(merged, "ctx", bit, 0)

    d_qkv_t = jnp.stack(pieces, axis=1).reshape(width, groups * rows)
    qkv_send, qkv_sum = qkv_grads(which, slots, d_qkv_t, fsdp)
    qkv_sum = add_low(qkv_sum, swap(qkv_send, "fsdp", 0))
    wide_sum = qkv_sum.astype(f32)
    for e in range(1, parts):
        wide_sum = wide_sum + part_shift(qkv_sum, groups, parts, e).astype(f32)
    qkv_sum, merged = together(wide_sum.astype(bf16), merged)
    other = swap(merged, "ctx", 0)
    late = send(late)
    for bit in fsdp_bits[1:]:
        qkv_sum = halve(qkv_sum, "fsdp", bit, 1)
    qkv_low = qkv_sum[0]
    qkv_full = gather_rest(qkv_held, qkv_top).reshape(model, 3 * model)
    by_group = jnp.zeros((groups,) + qkv_low.shape, bf16)
    turns = [ctx_swap(qkv_low, groups, parts, j) if j else qkv_low for j in range(groups)]
    other, *late = together(other, *late)
    turns = together(*turns)
    for j, piece in enumerate(turns):
        by_group = lax.dynamic_update_slice(by_group, piece[None], (g ^ j, 0, 0))
    natural = by_group.reshape(groups, shard + PAD, 3, span).transpose(1, 2, 0, 3)
    natural = natural.reshape(shard + PAD, 3 * model).astype(f32)
    grad_qkv_shard = natural[:shard]
    bias_line = natural[shard]
    grad_query_shift = lax.dynamic_slice(bias_line, (f * shard,), (shard,))
    grad_value_shift = lax.dynamic_slice(bias_line, (2 * model + f * shard,), (shard,))

    natural = jnp.zeros((3, groups, heads, HD, rows), bf16)
    for j in range(groups):
        part = jnp.stack([early[j], middle[j], late[j]], axis=1)[:, None]
        natural = lax.dynamic_update_slice(natural, part, (0, g ^ j, 0, 0, 0))
    input_grad = d_resid1 + lax.dot_general(
        natural.reshape(3 * model, rows),
        qkv_full,
        (((0,), (1,)), ((), ())),
        preferred_element_type=f32,
    )

    lower_rows = (inner_shard + shard + line_rows) // 2
    lower = join(bit_at("ctx", 0), merged[:lower_rows], other[:lower_rows], 0)
    wide_half = lambda m: jnp.concatenate(
        [m[lower_rows + c * shard : lower_rows + (c + 1) * shard] for c in range(chunks)], axis=1
    )
    upper = join(bit_at("ctx", 0), wide_half(merged), wide_half(other), 1)

    ends = inner_shard + shard
    flat = lower[ends:].reshape(-1).astype(f32)
    offsets = lambda i: flat[i * shard : (i + 1) * shard]
    return (
        result[None],
        input_grad[None],
        grad_qkv_shard,
        grad_query_shift,
        grad_value_shift,
        lower[inner_shard:ends].astype(f32),
        offsets(0),
        offsets(1),
        offsets(2),
        upper.astype(f32),
        flat[6 * shard : 6 * shard + inner_shard],
        lower[:inner_shard].astype(f32),
        offsets(3),
        offsets(4),
        offsets(5),
    )


def solution(mesh):
    rows, one = P("fsdp", None), P("fsdp")
    whole = P("fsdp", "ctx", None)
    return jax.shard_map(
        body,
        mesh=mesh,
        in_specs=(
            whole, rows, rows, one, one, rows, one, one, one, rows, one, rows, one, one, one, whole,
        ),
        out_specs=(
            whole, whole, rows, one, one, rows, one, one, one, rows, one, rows, one, one, one,
        ),
        check_vma=False,
    )
```

profile of v0, /device:TPU:8, one launch (start us, length us, event | category | flops | bytes accessed | tf_op | source)
XLA Modules:
  0.0 475.3 jit_solution(13689470992201881883)
XLA Ops:
  11.3 6.0 %collective-permute-done = bf16[208,576]{0,1:T(8,128)(2,1)S(1)} collective-permute-done((bf16[208,576]{0,1:T(8,128)(2,1)S(1)}, bf16[208,576]{0,1:T(8,128)(2,1)S(1)}, u32[]{:S(2)}, u32[]{:S(2)}) %collective-permute-start) | collective-permute-done | bytes 239648 | tf_op jit(solution)/shard_map/ppermute | solution.py:43
  35.1 9.2 %collective-permute-done.5.refs_4_ = bf16[2,3,64,512]{3,2,1,0:T(8,128)(2,1)S(1)} collective-permute-done((bf16[2,3,64,512]{3,2,1,0:T(8,128)(2,1)}, bf16[2,3,64,512]{3,2,1,0:T(8,128)(2,1)S(1)}, u32[]{:S(2)}, u32[]{:S(2)}) %collective-permute-start.5) | collective-permute-done | bytes 393248 | tf_op jit(solution)/shard_map/ppermute | solution.py:34
  66.3 5.8 %collective-permute-done.9.refs_3_ = bf16[512,768]{1,0:T(8,128)(2,1)} collective-permute-done((bf16[512,768]{1,0:T(8,128)(2,1)}, bf16[512,768]{1,0:T(8,128)(2,1)}, u32[]{:S(2)}, u32[]{:S(2)}) %collective-permute-start.9) | collective-permute-done | bytes 786464 | tf_op jit(solution)/shard_map/ppermute | solution.py:26
  92.5 36.4 %attend.1 = (bf16[3,64,2048]{2,1,0:T(8,128)(2,1)}, f32[3,64,2048]{2,1,0:T(8,128)}, f32[3,1,2048]{2,1,0:T(1,128)}) custom-call(s32[18]{0:T(128)} %pad_add_fusion.2.meta, bf16[3,3,64,512]{3,2,1,0:T(8,128)(2,1)} %bitcast.211, bf16[3,3,64,512]{3,2,1,0:T(8,128)(2,1)} %bitcast.215, bf16[3,3,64,512]{3,2,1,0:T(8,128)(2,1)} %bitcast.219, ...), custom_call_target="tpu_custom_call" | custom-call | flops 17999998976 | bytes 60000000 | tf_op jit(solution)/shard_map/attend/pallas_call | solution.py:290
  139.9 6.1 %collective-permute-done.14 = bf16[3,64,512]{2,1,0:T(8,128)(2,1)S(1)} collective-permute-done((bf16[3,64,512]{2,1,0:T(8,128)(2,1)S(1)}, bf16[3,64,512]{2,1,0:T(8,128)(2,1)S(1)}, u32[]{:S(2)}, u32[]{:S(2)}) %collective-permute-start.14) | collective-permute-done | bytes 196640 | tf_op jit(solution)/shard_map/ppermute | solution.py:26
  146.0 5.2 %collective-permute-done.15 = bf16[3,64,512]{2,1,0:T(8,128)(2,1)S(1)} collective-permute-done((bf16[3,64,512]{2,1,0:T(8,128)(2,1)S(1)}, bf16[3,64,512]{2,1,0:T(8,128)(2,1)S(1)}, u32[]{:S(2)}, u32[]{:S(2)}) %collective-permute-start.15) | collective-permute-done | bytes 196640 | tf_op jit(solution)/shard_map/ppermute | solution.py:26
  152.3 34.6 %feed_forward.1 = (bf16[512,768]{1,0:T(8,128)(2,1)}, f32[512,768]{1,0:T(8,128)}, bf16[768,512]{1,0:T(8,128)(2,1)}, bf16[4,512,192]{2,1,0:T(8,128)(2,1)}, bf16[4,...) custom-call(bf16[512,768]{1,0:T(8,128)(2,1)} %bitcast.254, ...), custom_call_target="tpu_custom_call" | custom-call | flops 10871635968 | bytes 30000000 | tf_op jit(solution)/shard_map/feed_forward/pallas_call | solution.py:485
  190.9 12.3 %weight_grads.1 = (bf16[2,1024,768]{2,1,0:T(8,128)(2,1)}, bf16[2,192,3072]{2,1,0:T(8,128)(2,1)}, bf16[2,1024,768]{2,1,0:T(8,128)(2,1)}, bf16[2,192,3072]{2,1,0:T(8,128)(2,1)}) custom-call(s32[2]{0:T(128)} %pad_add_fusion.3.which, bf16[4,512,768]{2,1,0:T(8,128)(2,1)} %get-tuple-element.121.refs_0_.refs_4_, ...), custom_call_target="tpu_custom_call" | custom-call | flops 5435817984 | bytes 25000000 | tf_op jit(solution)/shard_map/weight_grads/pallas_call | solution.py:542
  220.4 5.3 %collective-permute-start.20 = (bf16[1,1024,768]{2,1,0:T(8,128)(2,1)}, bf16[1,1024,768]{2,1,0:T(8,128)(2,1)}, u32[]{:S(2)}, u32[]{:S(2)}) collective-permute-start(bf16[1,1024,768]{2,1,0:T(8,128)(2,1)} %constant_dynamic-slice_fusion.11), channel_id=1, source_target_pairs={{0,2},{1,3},{2,0},{3,1},{4,6},{5,7},{6,4},{7,5},{8,10},{9,11},{10,... | collective-permute-start | bytes 4718600 | tf_op jit(solution)/shard_map/ppermute | solution.py:43
  228.3 17.0 %attend_back.5 = (bf16[64,2048]{1,0:T(8,128)(2,1)}, f32[2,64,2048]{2,1,0:T(8,128)}, bf16[1,2,64,2048]{3,2,1,0:T(8,128)(2,1)}) custom-call(s32[18]{0:T(128)} %pad_add_fusion.2.meta, bf16[3,3,64,512]{3,2,1,0:T(8,128)(2,1)} %bitcast.212, bf16[3,3,64,512]{3,2,1,0:T(8,128)(2,1)} %bitcast.216, bf16[3,3,64,512]{3,2,1,0:T(8,128)(2,1)} %bitcast.220, ...), custom_call_target="tpu_custom_call" | custom-call | flops 15000000512 | bytes 20000000 | tf_op jit(solution)/shard_map/attend_back/pallas_call | solution.py:337
  249.5 10.7 %collective-permute-done.20 = bf16[1,1024,768]{2,1,0:T(8,128)(2,1)} collective-permute-done((bf16[1,1024,768]{2,1,0:T(8,128)(2,1)}, bf16[1,1024,768]{2,1,0:T(8,128)(2,1)}, u32[]{:S(2)}, u32[]{:S(2)}) %collective-permute-start.20) | collective-permute-done | bytes 1572896 | tf_op jit(solution)/shard_map/ppermute | solution.py:43
  265.4 16.9 %attend_back.3 = (bf16[64,2048]{1,0:T(8,128)(2,1)}, f32[2,64,2048]{2,1,0:T(8,128)}, bf16[1,2,64,2048]{3,2,1,0:T(8,128)(2,1)}) custom-call(s32[18]{0:T(128)} %pad_add_fusion.2.meta, bf16[3,3,64,512]{3,2,1,0:T(8,128)(2,1)} %bitcast.213, bf16[3,3,64,512]{3,2,1,0:T(8,128)(2,1)} %bitcast.217, bf16[3,3,64,512]{3,2,1,0:T(8,128)(2,1)} %bitcast.221, ...), custom_call_target="tpu_custom_call" | custom-call | flops 15000000512 | bytes 20000000 | tf_op jit(solution)/shard_map/attend_back/pallas_call | solution.py:337
  293.7 17.2 %attend_back.4 = (bf16[64,2048]{1,0:T(8,128)(2,1)}, f32[2,64,2048]{2,1,0:T(8,128)}, bf16[1,2,64,2048]{3,2,1,0:T(8,128)(2,1)}) custom-call(s32[18]{0:T(128)} %pad_add_fusion.2.meta, bf16[3,3,64,512]{3,2,1,0:T(8,128)(2,1)} %bitcast.214, bf16[3,3,64,512]{3,2,1,0:T(8,128)(2,1)} %bitcast.218, bf16[3,3,64,512]{3,2,1,0:T(8,128)(2,1)} %bitcast.222, ...), custom_call_target="tpu_custom_call" | custom-call | flops 15000000512 | bytes 20000000 | tf_op jit(solution)/shard_map/attend_back/pallas_call | solution.py:337
  310.9 5.9 %collective-permute-done.27 = bf16[448,768]{1,0:T(8,128)(2,1)} collective-permute-done((bf16[448,768]{1,0:T(8,128)(2,1)}, bf16[448,768]{1,0:T(8,128)(2,1)}, u32[]{:S(2)}, u32[]{:S(2)}) %collective-permute-start.27) | collective-permute-done | bytes 688160 | tf_op jit(solution)/shard_map/ppermute | solution.py:43
  327.4 9.3 %collective-permute-done.30 = bf16[192,2304]{1,0:T(8,128)(2,1)S(1)} collective-permute-done((bf16[192,2304]{1,0:T(8,128)(2,1)S(1)}, bf16[192,2304]{1,0:T(8,128)(2,1)S(1)}, u32[]{:S(2)}, u32[]{:S(2)}) %collective-permute-start.30) | collective-permute-done | bytes 884768 | tf_op jit(solution)/shard_map/ppermute | solution.py:43
  338.6 14.3 %collective-permute-done.36 = bf16[3,64,512]{2,1,0:T(8,128)(2,1)S(1)} collective-permute-done((bf16[3,64,512]{2,1,0:T(8,128)(2,1)S(1)}, bf16[3,64,512]{2,1,0:T(8,128)(2,1)S(1)}, u32[]{:S(2)}, u32[]{:S(2)}) %collective-permute-start.36) | collective-permute-done | bytes 196640 | tf_op jit(solution)/shard_map/ppermute | solution.py:26
  352.9 5.8 %collective-permute-done.37 = bf16[3,64,512]{2,1,0:T(8,128)(2,1)S(1)} collective-permute-done((bf16[3,64,512]{2,1,0:T(8,128)(2,1)S(1)}, bf16[3,64,512]{2,1,0:T(8,128)(2,1)S(1)}, u32[]{:S(2)}, u32[]{:S(2)}) %collective-permute-start.37) | collective-permute-done | bytes 196640 | tf_op jit(solution)/shard_map/ppermute | solution.py:26
  358.7 11.6 %collective-permute-done.34 = bf16[448,768]{1,0:T(8,128)(2,1)S(1)} collective-permute-done((bf16[448,768]{1,0:T(8,128)(2,1)S(1)}, bf16[448,768]{1,0:T(8,128)(2,1)S(1)}, u32[]{:S(2)}, u32[]{:S(2)}) %collective-permute-start.34) | collective-permute-done | bytes 688160 | tf_op jit(solution)/shard_map/ppermute | solution.py:43
  373.0 7.6 %qkv_grads.1 = (bf16[2,208,576]{2,1,0:T(8,128)(2,1)}, bf16[2,208,576]{2,1,0:T(8,128)(2,1)}) custom-call(s32[2]{0:T(128)} %pad_add_fusion.3.which, bf16[512,768]{1,0:T(8,128)(2,1)} %bitcast.255, bf16[512,768]{1,0:T(8,128)(2,1)} %collective-permute-done.7.refs_1_, bf16[512,768]{1,0:T(8,128)(2,1)} %collective-permute-done.8.refs_2_, ...), custom_call_target="tpu_custom_call" | custom-call | flops 1811939328 | bytes 8000000 | tf_op jit(solution)/shard_map/qkv_grads/pallas_call | solution.py:581
  387.1 13.6 %collective-permute-done.41 = bf16[448,768]{1,0:T(8,128)(2,1)S(1)} collective-permute-done((bf16[448,768]{1,0:T(8,128)(2,1)S(1)}, bf16[448,768]{1,0:T(8,128)(2,1)S(1)}, u32[]{:S(2)}, u32[]{:S(2)}) %collective-permute-start.41) | collective-permute-done | bytes 688160 | tf_op jit(solution)/shard_map/ppermute | solution.py:43
  408.9 4.4 collective-permute-done.47
  419.0 4.3 collective-permute-done.48
  426.2 14.5 %collective-permute-done.49 = bf16[208,576]{1,0:T(8,128)(2,1)S(1)} collective-permute-done((bf16[208,576]{1,0:T(8,128)(2,1)S(1)}, bf16[208,576]{1,0:T(8,128)(2,1)S(1)}, u32[]{:S(2)}, u32[]{:S(2)}) %collective-permute-start.49) | collective-permute-done | bytes 239648 | tf_op jit(solution)/shard_map/ppermute | solution.py:26
  441.4 8.3 %collective-permute-done.50 = bf16[208,576]{1,0:T(8,128)(2,1)S(1)} collective-permute-done((bf16[208,576]{1,0:T(8,128)(2,1)S(1)}, bf16[208,576]{1,0:T(8,128)(2,1)S(1)}, u32[]{:S(2)}, u32[]{:S(2)}) %collective-permute-start.50) | collective-permute-done | bytes 239648 | tf_op jit(solution)/shard_map/ppermute | solution.py:26
  (368 shorter events, 190.8 us)
Async XLA Ops:
  0.6 60.2 %collective-permute-start.7 = (bf16[512,768]{1,0:T(8,128)(2,1)}, bf16[512,768]{1,0:T(8,128)(2,1)}, u32[]{:S(2)}, u32[]{:S(2)}) collective-permute-start(bf16[512,768]{1,0:T(8,128)(2,1)} %bitcast.251), channel_id=1, source_target_pairs={{0,8},{4,12},{8,0},{12,4},{16,24},{20,28},{24,16},{28,20},{1,9},{5... | collective-permute-start | bytes 2359304 | tf_op jit(solution)/shard_map/ppermute | solution.py:26
  0.7 62.1 %collective-permute-start.8 = (bf16[512,768]{1,0:T(8,128)(2,1)}, bf16[512,768]{1,0:T(8,128)(2,1)}, u32[]{:S(2)}, u32[]{:S(2)}) collective-permute-start(bf16[512,768]{1,0:T(8,128)(2,1)} %bitcast.252), channel_id=1, source_target_pairs={{0,16},{4,20},{8,24},{12,28},{16,0},{20,4},{24,8},{28,12},{1,17},{... | collective-permute-start | bytes 2359304 | tf_op jit(solution)/shard_map/ppermute | solution.py:26
  3.8 68.4 %collective-permute-start.9 = (bf16[512,768]{1,0:T(8,128)(2,1)}, bf16[512,768]{1,0:T(8,128)(2,1)}, u32[]{:S(2)}, u32[]{:S(2)}) collective-permute-start(bf16[512,768]{1,0:T(8,128)(2,1)} %bitcast.253), channel_id=1, source_target_pairs={{0,24},{4,28},{8,16},{12,20},{16,8},{20,12},{24,0},{28,4},{1,25},{... | collective-permute-start | bytes 2359304 | tf_op jit(solution)/shard_map/ppermute | solution.py:26
  18.2 28.6 %collective-permute-start.3 = (bf16[192,3072]{1,0:T(8,128)(2,1)S(1)}, bf16[192,3072]{1,0:T(8,128)(2,1)S(1)}, u32[]{:S(2)}, u32[]{:S(2)}) collective-permute-start(bf16[192,3072]{1,0:T(8,128)(2,1)S(1)} %copy-done.5), channel_id=1, source_target_pairs={{0,2},{1,3},{2,0},{3,1},{4,6},{5,7},{6,4},{7,5},{8,10},{9,11},{10,... | collective-permute-start | bytes 3538952 | tf_op jit(solution)/shard_map/ppermute | solution.py:43
  48.5 36.3 %collective-permute-start.6 = (bf16[2,192,3072]{2,1,0:T(8,128)(2,1)}, bf16[2,192,3072]{2,1,0:T(8,128)(2,1)}, u32[]{:S(2)}, u32[]{:S(2)}) collective-permute-start(bf16[2,192,3072]{2,1,0:T(8,128)(2,1)} %maximum_select_fusion.4), channel_id=1, source_target_pairs={{0,1},{1,0},{2,3},{3,2},{4,5},{5,4},{6,7},{7,6},{8,9},{9,8},{10,11... | collective-permute-start | bytes 7077896 | tf_op jit(solution)/shard_map/ppermute | solution.py:43
  53.0 27.3 %collective-permute-start.16 = (bf16[768,768]{1,0:T(8,128)(2,1)S(1)}, bf16[768,768]{1,0:T(8,128)(2,1)S(1)}, u32[]{:S(2)}, u32[]{:S(2)}) collective-permute-start(bf16[768,768]{1,0:T(8,128)(2,1)S(1)} %copy-done.4), channel_id=1, source_target_pairs={{0,2},{1,3},{2,0},{3,1},{4,6},{5,7},{6,4},{7,5},{8,10},{9,11},{10,... | collective-permute-start | bytes 3538952 | tf_op jit(solution)/shard_map/ppermute | solution.py:43
  62.8 28.1 %collective-permute-start.10 = (bf16[2,3,64,512]{3,2,1,0:T(8,128)(2,1)S(1)}, bf16[2,3,64,512]{3,2,1,0:T(8,128)(2,1)S(1)}, u32[]{:S(2)}, u32[]{:S(2)}) collective-permute-start(bf16[2,3,64,512]{3,2,1,0:T(8,128)(2,1)S(1)} %bitcast.205), channel_id=1, source_target_pairs={{0,4},{4,0},{8,12},{12,8},{16,20},{20,16},{24,28},{28,24},{1,5},{5... | collective-permute-start | bytes 1179656 | tf_op jit(solution)/shard_map/ppermute | solution.py:34
  82.1 52.2 %collective-permute-start.17 = (bf16[2,768,768]{2,1,0:T(8,128)(2,1)}, bf16[2,768,768]{2,1,0:T(8,128)(2,1)}, u32[]{:S(2)}, u32[]{:S(2)}) collective-permute-start(bf16[2,768,768]{2,1,0:T(8,128)(2,1)} %maximum_select_fusion.6), channel_id=1, source_target_pairs={{0,1},{1,0},{2,3},{3,2},{4,5},{5,4},{6,7},{7,6},{8,9},{9,8},{10,11... | collective-permute-start | bytes 7077896 | tf_op jit(solution)/shard_map/ppermute | solution.py:43
  219.2 28.4 %collective-permute-start.21 = (bf16[2,192,1536]{2,1,0:T(8,128)(2,1)}, bf16[2,192,1536]{2,1,0:T(8,128)(2,1)}, u32[]{:S(2)}, u32[]{:S(2)}) collective-permute-start(bf16[2,192,1536]{2,1,0:T(8,128)(2,1)} %constant_dynamic-slice_fusion.10), channel_id=1, source_target_pairs={{0,4},{4,0},{8,12},{12,8},{16,20},{20,16},{24,28},{28,24},{1,5},{5... | collective-permute-start | bytes 3538952 | tf_op jit(solution)/shard_map/ppermute | solution.py:43
  220.4 39.7 %collective-permute-start.20 = (bf16[1,1024,768]{2,1,0:T(8,128)(2,1)}, bf16[1,1024,768]{2,1,0:T(8,128)(2,1)}, u32[]{:S(2)}, u32[]{:S(2)}) collective-permute-start(bf16[1,1024,768]{2,1,0:T(8,128)(2,1)} %constant_dynamic-slice_fusion.11), channel_id=1, source_target_pairs={{0,2},{1,3},{2,0},{3,1},{4,6},{5,7},{6,4},{7,5},{8,10},{9,11},{10,... | collective-permute-start | bytes 4718600 | tf_op jit(solution)/shard_map/ppermute | solution.py:43
  245.3 38.9 %collective-permute-start.29 = (bf16[2,64,2048]{2,1,0:T(8,128)(2,1)}, bf16[2,64,2048]{2,1,0:T(8,128)(2,1)}, u32[]{:S(2)}, u32[]{:S(2)}) collective-permute-start(bf16[2,64,2048]{2,1,0:T(8,128)(2,1)} %bitcast.257), channel_id=1, source_target_pairs={{0,4},{4,0},{8,12},{12,8},{16,20},{20,16},{24,28},{28,24},{1,5},{5... | collective-permute-start | bytes 1572872 | tf_op jit(solution)/shard_map/ppermute | solution.py:34
  287.3 36.5 %collective-permute-start.31 = (bf16[3,64,512]{2,1,0:T(8,128)(2,1)}, bf16[3,64,512]{2,1,0:T(8,128)(2,1)}, u32[]{:S(2)}, u32[]{:S(2)}) collective-permute-start(bf16[3,64,512]{2,1,0:T(8,128)(2,1)} %get-tuple-element.207), channel_id=1, source_target_pairs={{0,8},{4,12},{8,0},{12,4},{16,24},{20,28},{24,16},{28,20},{1,9},{5... | collective-permute-start | bytes 589832 | tf_op jit(solution)/shard_map/ppermute | solution.py:26
  288.1 36.1 %collective-permute-start.32 = (bf16[3,64,512]{2,1,0:T(8,128)(2,1)S(1)}, bf16[3,64,512]{2,1,0:T(8,128)(2,1)}, u32[]{:S(2)}, u32[]{:S(2)}) collective-permute-start(bf16[3,64,512]{2,1,0:T(8,128)(2,1)S(1)} %get-tuple-element.208), channel_id=1, source_target_pairs={{0,16},{4,20},{8,24},{12,28},{16,0},{20,4},{24,8},{28,12},{1,17},{... | collective-permute-start | bytes 589832 | tf_op jit(solution)/shard_map/ppermute | solution.py:26
  290.4 36.4 %collective-permute-start.33 = (bf16[3,64,512]{2,1,0:T(8,128)(2,1)S(1)}, bf16[3,64,512]{2,1,0:T(8,128)(2,1)}, u32[]{:S(2)}, u32[]{:S(2)}) collective-permute-start(bf16[3,64,512]{2,1,0:T(8,128)(2,1)S(1)} %get-tuple-element.205), channel_id=1, source_target_pairs={{0,24},{4,28},{8,16},{12,20},{16,8},{20,12},{24,0},{28,4},{1,25},{... | collective-permute-start | bytes 589832 | tf_op jit(solution)/shard_map/ppermute | solution.py:26
  293.4 25.4 %collective-permute-start.28 = (bf16[2,64,2048]{2,1,0:T(8,128)(2,1)}, bf16[2,64,2048]{2,1,0:T(8,128)(2,1)}, u32[]{:S(2)}, u32[]{:S(2)}) collective-permute-start(bf16[2,64,2048]{2,1,0:T(8,128)(2,1)} %bitcast.57), channel_id=1, source_target_pairs={{0,4},{4,0},{8,12},{12,8},{16,20},{20,16},{24,28},{28,24},{1,5},{5... | collective-permute-start | bytes 1572872 | tf_op jit(solution)/shard_map/ppermute | solution.py:34
  324.2 28.7 %collective-permute-start.36 = (bf16[3,64,512]{2,1,0:T(8,128)(2,1)S(1)}, bf16[3,64,512]{2,1,0:T(8,128)(2,1)S(1)}, u32[]{:S(2)}, u32[]{:S(2)}) collective-permute-start(bf16[3,64,512]{2,1,0:T(8,128)(2,1)S(1)} %get-tuple-element.212), channel_id=1, source_target_pairs={{0,16},{4,20},{8,24},{12,28},{16,0},{20,4},{24,8},{28,12},{1,17},{... | collective-permute-start | bytes 589832 | tf_op jit(solution)/shard_map/ppermute | solution.py:26
  326.8 31.8 %collective-permute-start.37 = (bf16[3,64,512]{2,1,0:T(8,128)(2,1)S(1)}, bf16[3,64,512]{2,1,0:T(8,128)(2,1)S(1)}, u32[]{:S(2)}, u32[]{:S(2)}) collective-permute-start(bf16[3,64,512]{2,1,0:T(8,128)(2,1)S(1)} %get-tuple-element.209), channel_id=1, source_target_pairs={{0,24},{4,28},{8,16},{12,20},{16,8},{20,12},{24,0},{28,4},{1,25},{... | collective-permute-start | bytes 589832 | tf_op jit(solution)/shard_map/ppermute | solution.py:26
  336.7 33.6 %collective-permute-start.34 = (bf16[448,768]{1,0:T(8,128)(2,1)S(1)}, bf16[448,768]{1,0:T(8,128)(2,1)S(1)}, u32[]{:S(2)}, u32[]{:S(2)}) collective-permute-start(bf16[448,768]{1,0:T(8,128)(2,1)S(1)} %add_convert_fusion.6), channel_id=1, source_target_pairs={{0,16},{4,20},{8,24},{12,28},{16,0},{20,4},{24,8},{28,12},{1,17},{... | collective-permute-start | bytes 2064392 | tf_op jit(solution)/shard_map/ppermute | solution.py:43
  380.9 35.5 %collective-permute-start.46 = (bf16[2,192,2304]{2,1,0:T(8,128)(2,1)S(1)}, bf16[2,192,2304]{2,1,0:T(8,128)(2,1)S(1)}, u32[]{:S(2)}, u32[]{:S(2)}) collective-permute-start(bf16[2,192,2304]{2,1,0:T(8,128)(2,1)S(1)} %maximum_select_fusion.8), channel_id=1, source_target_pairs={{0,1},{1,0},{2,3},{3,2},{4,5},{5,4},{6,7},{7,6},{8,9},{9,8},{10,11... | collective-permute-start | bytes 5308424 | tf_op jit(solution)/shard_map/ppermute | solution.py:43
  386.5 72.3 %collective-permute-start.43 = (bf16[3,64,512]{2,1,0:T(8,128)(2,1)}, bf16[3,64,512]{2,1,0:T(8,128)(2,1)}, u32[]{:S(2)}, u32[]{:S(2)}) collective-permute-start(bf16[3,64,512]{2,1,0:T(8,128)(2,1)} %get-tuple-element.203), channel_id=1, source_target_pairs={{0,8},{4,12},{8,0},{12,4},{16,24},{20,28},{24,16},{28,20},{1,9},{5... | collective-permute-start | bytes 589832 | tf_op jit(solution)/shard_map/ppermute | solution.py:26
  402.5 56.3 %collective-permute-start.42 = (bf16[896,768]{1,0:T(8,128)(2,1)}, bf16[896,768]{1,0:T(8,128)(2,1)}, u32[]{:S(2)}, u32[]{:S(2)}) collective-permute-start(bf16[896,768]{1,0:T(8,128)(2,1)} %maximum_select_fusion.10), channel_id=1, source_target_pairs={{0,4},{4,0},{8,12},{12,8},{16,20},{20,16},{24,28},{28,24},{1,5},{5... | collective-permute-start | bytes 4128776 | tf_op jit(solution)/shard_map/ppermute | solution.py:43
  414.8 25.9 %collective-permute-start.49 = (bf16[208,576]{1,0:T(8,128)(2,1)S(1)}, bf16[208,576]{1,0:T(8,128)(2,1)S(1)}, u32[]{:S(2)}, u32[]{:S(2)}) collective-permute-start(bf16[208,576]{1,0:T(8,128)(2,1)S(1)} %fusion.6), channel_id=1, source_target_pairs={{0,16},{4,20},{8,24},{12,28},{16,0},{20,4},{24,8},{28,12},{1,17},{... | collective-permute-start | bytes 718856 | tf_op jit(solution)/shard_map/ppermute | solution.py:26
  416.4 33.2 %collective-permute-start.50 = (bf16[208,576]{1,0:T(8,128)(2,1)S(1)}, bf16[208,576]{1,0:T(8,128)(2,1)S(1)}, u32[]{:S(2)}, u32[]{:S(2)}) collective-permute-start(bf16[208,576]{1,0:T(8,128)(2,1)S(1)} %fusion.6), channel_id=1, source_target_pairs={{0,24},{4,28},{8,16},{12,20},{16,8},{20,12},{24,0},{28,4},{1,25},{... | collective-permute-start | bytes 718856 | tf_op jit(solution)/shard_map/ppermute | solution.py:26
  423.2 35.6 %collective-permute-start.44 = (bf16[3,64,512]{2,1,0:T(8,128)(2,1)}, bf16[3,64,512]{2,1,0:T(8,128)(2,1)}, u32[]{:S(2)}, u32[]{:S(2)}) collective-permute-start(bf16[3,64,512]{2,1,0:T(8,128)(2,1)} %get-tuple-element.202), channel_id=1, source_target_pairs={{0,16},{4,20},{8,24},{12,28},{16,0},{20,4},{24,8},{28,12},{1,17},{... | collective-permute-start | bytes 589832 | tf_op jit(solution)/shard_map/ppermute | solution.py:26
  (95 other events, 765.7 us)
where the time goes:
time: 484 us; the launch traced here: 475 us
  waiting for transfers between devices  148 us (31%)
  Pallas kernels  142 us (29%)
  local copies, waits for them, and re-layouts  58.8 us (12%)
  starting transfers between devices  58.7 us (12%)
  other arithmetic  54.7 us (11%)
  matrix products  10.7 us (2%)
    ppermute x22, waiting for transfers between devices, swap(): return lax.ppermute(array, axis, [(i, i ^ 1 << bit) for i in range(size)])  72.4 us
    ppermute x21, waiting for transfers between devices, ctx_swap(): return lax.ppermute(array, 'ctx', pairs)  66.2 us
    pallas_call x3, Pallas kernels, attend_back(): pl.pallas_call(partial(attend_back_kernel, groups, parts, docs, rows), gr...  51 us
    pallas_call x1, Pallas kernels, attend(): pl.pallas_call(partial(attend_kernel, groups, parts, docs, rows), grid_sp...  36.4 us
    pallas_call x1, Pallas kernels, feed_forward(): pl.pallas_call(feed_kernel, grid=(rows // tile,), in_specs=[by_rows(model...  34.6 us
    ppermute x21, starting transfers between devices, ctx_swap(): return lax.ppermute(array, 'ctx', pairs)  26 us
    select_n x17, other arithmetic, join(): jnp.where(mine == 0, jnp.concatenate([own, other], axis=dim), jnp.concate...  25.4 us
    ppermute x22, starting transfers between devices, swap(): return lax.ppermute(array, axis, [(i, i ^ 1 << bit) for i in range(size)])  23.5 us
  transfers between devices with their start and end apart: 51, of which 22 were waited for; matrix products, arithmetic and copies ran while one was open for 19% of the time, Pallas kernels for 18%

commit v1 on v0

--- a/solution.py
+++ b/solution.py
@@ -788,34 +788,33 @@
             qkv_top = gather_top(qkv_held)
         elif head == 2:
             middle = send(pieces[1])
-            dq, qkv_top, *early = together(dq, qkv_top, *early)
+            dq, *early = together(dq, *early)
         held = (dq, dkv)
         theirs = [part_shift(rest[0][e - 1], groups, parts, -e) for e in range(1, parts)]
     settle(*held, theirs)
     for advance in steps:
         state = advance(state)
     other = swap(state[0], "ctx", ctx_bits[-1])
-    count = len(middle)
-    other, *landed = together(other, *middle, *pieces)
-    middle, pieces = landed[:count], landed[count:]
+    d_qkv_t = jnp.stack(pieces, axis=1).reshape(width, groups * rows)
+    qkv_send, qkv_sum = qkv_grads(which, slots, d_qkv_t, fsdp)
+    other, qkv_send, qkv_sum, qkv_top, *middle = together(
+        other, qkv_send, qkv_sum, qkv_top, *middle
+    )
+    qkv_full = gather_rest(qkv_held, qkv_top).reshape(model, 3 * model)
     merged = add_low(state[0], other)
     late, merged = together(pieces[2], merged)
     for bit in reversed(ctx_bits[1:-1]):
         merged = double(merged, "ctx", bit, 0)
-
-    d_qkv_t = jnp.stack(pieces, axis=1).reshape(width, groups * rows)
-    qkv_send, qkv_sum = qkv_grads(which, slots, d_qkv_t, fsdp)
     qkv_sum = add_low(qkv_sum, swap(qkv_send, "fsdp", 0))
     wide_sum = qkv_sum.astype(f32)
     for e in range(1, parts):
         wide_sum = wide_sum + part_shift(qkv_sum, groups, parts, e).astype(f32)
-    qkv_sum, merged = together(wide_sum.astype(bf16), merged)
+    qkv_sum, merged, qkv_full = together(wide_sum.astype(bf16), merged, qkv_full)
     other = swap(merged, "ctx", 0)
     late = send(late)
     for bit in fsdp_bits[1:]:
         qkv_sum = halve(qkv_sum, "fsdp", bit, 1)
     qkv_low = qkv_sum[0]
-    qkv_full = gather_rest(qkv_held, qkv_top).reshape(model, 3 * model)
     by_group = jnp.zeros((groups,) + qkv_low.shape, bf16)
     turns = [ctx_swap(qkv_low, groups, parts, j) if j else qkv_low for j in range(groups)]
     other, *late = together(other, *late)

time: 484 us -> 467 us (0.965)
  waiting for transfers between devices: 148 us -> 118 us
  starting transfers between devices: 58.7 us -> 88.5 us
  Pallas kernels: 142 us -> 121 us
  other arithmetic: 54.7 us -> 63.9 us
    ppermute x22, waiting for transfers between devices: 72.4 us -> 51.1 us  [swap(): return lax.ppermute(array, axis, [(i, i ^ 1 << bit) for i in range(size)])]
    ppermute x22, starting transfers between devices: 23.5 us -> 44.4 us  [swap(): return lax.ppermute(array, axis, [(i, i ^ 1 << bit) for i in range(size)])]
    ppermute x21, waiting for transfers between devices: 66.2 us -> 52.5 us  [ctx_swap(): return lax.ppermute(array, 'ctx', pairs)]
    pallas_call x3, Pallas kernels: 51 us -> 39.8 us  [attend_back(): pl.pallas_call(partial(attend_back_kernel, groups, parts, docs, rows), gr...]
    pallas_call x1, Pallas kernels: 36.4 us -> 26.5 us  [attend(): pl.pallas_call(partial(attend_kernel, groups, parts, docs, rows), grid_sp...]
    ppermute x8, starting transfers between devices: 9.23 us -> 15.9 us  [part_shift(): return lax.ppermute(array, 'ctx', pairs)]
    ppermute x8, waiting for transfers between devices: 9.48 us -> 14.6 us  [part_shift(): return lax.ppermute(array, 'ctx', pairs)]
    unnamed x140 -> x130, local copies, waits for them, and re-layouts: 13.2 us -> 10.1 us
  transfers between devices with their start and end apart: 51 -> 51, of which waited for: 22 -> 22; matrix products, arithmetic and copies ran while one was open for 19% -> 21% of each run, Pallas kernels for 18% -> 16%
where the time goes in v1:
time: 467 us; the launch traced here: 460 us
  Pallas kernels  121 us (26%)
  waiting for transfers between devices  118 us (25%)
  starting transfers between devices  88.5 us (19%)
  other arithmetic  63.9 us (14%)
  local copies, waits for them, and re-layouts  55.8 us (12%)
  matrix products  10.7 us (2%)
    ppermute x21, waiting for transfers between devices, ctx_swap(): return lax.ppermute(array, 'ctx', pairs)  52.5 us
    ppermute x22, waiting for transfers between devices, swap(): return lax.ppermute(array, axis, [(i, i ^ 1 << bit) for i in range(size)])  51.1 us
    ppermute x22, starting transfers between devices, swap(): return lax.ppermute(array, axis, [(i, i ^ 1 << bit) for i in range(size)])  44.4 us
    pallas_call x3, Pallas kernels, attend_back(): pl.pallas_call(partial(attend_back_kernel, groups, parts, docs, rows), gr...  39.8 us
    pallas_call x1, Pallas kernels, feed_forward(): pl.pallas_call(feed_kernel, grid=(rows // tile,), in_specs=[by_rows(model...  34.6 us
    select_n x17, other arithmetic, join(): jnp.where(mine == 0, jnp.concatenate([own, other], axis=dim), jnp.concate...  29.8 us
    ppermute x21, starting transfers between devices, ctx_swap(): return lax.ppermute(array, 'ctx', pairs)  28.1 us
    pallas_call x1, Pallas kernels, attend(): pl.pallas_call(partial(attend_kernel, groups, parts, docs, rows), grid_sp...  26.5 us
  transfers between devices with their start and end apart: 51, of which 22 were waited for; matrix products, arithmetic and copies ran while one was open for 21% of the time, Pallas kernels for 16%

profile of v1, /device:TPU:8, one launch (start us, length us, event | category | flops | bytes accessed | tf_op | source)
XLA Modules:
  0.0 460.3 jit_solution(4302877080940571386)
XLA Ops:
  11.3 6.0 %collective-permute-done = bf16[208,576]{0,1:T(8,128)(2,1)S(1)} collective-permute-done((bf16[208,576]{0,1:T(8,128)(2,1)S(1)}, bf16[208,576]{0,1:T(8,128)(2,1)S(1)}, u32[]{:S(2)}, u32[]{:S(2)}) %collective-permute-start) | collective-permute-done | bytes 239648 | tf_op jit(solution)/shard_map/ppermute | solution.py:43
  35.1 9.2 %collective-permute-done.5.refs_4_ = bf16[2,3,64,512]{3,2,1,0:T(8,128)(2,1)S(1)} collective-permute-done((bf16[2,3,64,512]{3,2,1,0:T(8,128)(2,1)}, bf16[2,3,64,512]{3,2,1,0:T(8,128)(2,1)S(1)}, u32[]{:S(2)}, u32[]{:S(2)}) %collective-permute-start.5) | collective-permute-done | bytes 393248 | tf_op jit(solution)/shard_map/ppermute | solution.py:34
  66.3 5.8 %collective-permute-done.9.refs_3_ = bf16[512,768]{1,0:T(8,128)(2,1)} collective-permute-done((bf16[512,768]{1,0:T(8,128)(2,1)}, bf16[512,768]{1,0:T(8,128)(2,1)}, u32[]{:S(2)}, u32[]{:S(2)}) %collective-permute-start.9) | collective-permute-done | bytes 786464 | tf_op jit(solution)/shard_map/ppermute | solution.py:26
  92.4 26.5 %attend.1 = (bf16[3,64,2048]{2,1,0:T(8,128)(2,1)}, f32[3,64,2048]{2,1,0:T(8,128)}, f32[3,1,2048]{2,1,0:T(1,128)}) custom-call(s32[18]{0:T(128)} %pad_add_fusion.2.meta, bf16[3,3,64,512]{3,2,1,0:T(8,128)(2,1)} %bitcast.211, bf16[3,3,64,512]{3,2,1,0:T(8,128)(2,1)} %bitcast.215, bf16[3,3,64,512]{3,2,1,0:T(8,128)(2,1)} %bitcast.219, ...), custom_call_target="tpu_custom_call" | custom-call | flops 17999998976 | bytes 60000000 | tf_op jit(solution)/shard_map/attend/pallas_call | solution.py:290
  135.4 34.6 %feed_forward.1 = (bf16[512,768]{1,0:T(8,128)(2,1)}, f32[512,768]{1,0:T(8,128)}, bf16[768,512]{1,0:T(8,128)(2,1)}, bf16[4,512,192]{2,1,0:T(8,128)(2,1)}, bf16[4,...) custom-call(bf16[512,768]{1,0:T(8,128)(2,1)} %bitcast.252, ...), custom_call_target="tpu_custom_call" | custom-call | flops 10871635968 | bytes 30000000 | tf_op jit(solution)/shard_map/feed_forward/pallas_call | solution.py:485
  174.0 12.3 %weight_grads.1 = (bf16[2,1024,768]{2,1,0:T(8,128)(2,1)}, bf16[2,192,3072]{2,1,0:T(8,128)(2,1)}, bf16[2,1024,768]{2,1,0:T(8,128)(2,1)}, bf16[2,192,3072]{2,1,0:T(8,128)(2,1)}) custom-call(s32[2]{0:T(128)} %pad_add_fusion.3.which, bf16[4,512,768]{2,1,0:T(8,128)(2,1)} %get-tuple-element.121.refs_0_.refs_4_, ...), custom_call_target="tpu_custom_call" | custom-call | flops 5435817984 | bytes 25000000 | tf_op jit(solution)/shard_map/weight_grads/pallas_call | solution.py:542
  186.3 15.2 %collective-permute-start.19 = (bf16[2,192,3072]{2,1,0:T(8,128)(2,1)}, bf16[2,192,3072]{2,1,0:T(8,128)(2,1)}, u32[]{:S(2)}, u32[]{:S(2)}) collective-permute-start(bf16[2,192,3072]{2,1,0:T(8,128)(2,1)} %get-tuple-element.131), channel_id=1, source_target_pairs={{0,1},{1,0},{2,3},{3,2},{4,5},{5,4},{6,7},{7,6},{8,9},{9,8},{10,11... | collective-permute-start | bytes 7077896 | tf_op jit(solution)/shard_map/ppermute | solution.py:43
  225.3 13.2 %attend_back.5 = (bf16[64,2048]{1,0:T(8,128)(2,1)}, f32[2,64,2048]{2,1,0:T(8,128)}, bf16[1,2,64,2048]{3,2,1,0:T(8,128)(2,1)}) custom-call(s32[18]{0:T(128)} %pad_add_fusion.2.meta, bf16[3,3,64,512]{3,2,1,0:T(8,128)(2,1)} %bitcast.212, bf16[3,3,64,512]{3,2,1,0:T(8,128)(2,1)} %bitcast.216, bf16[3,3,64,512]{3,2,1,0:T(8,128)(2,1)} %bitcast.220, ...), custom_call_target="tpu_custom_call" | custom-call | flops 15000000512 | bytes 20000000 | tf_op jit(solution)/shard_map/attend_back/pallas_call | solution.py:337
  238.5 5.5 %collective-permute-start.29 = (bf16[2,64,2048]{2,1,0:T(8,128)(2,1)}, bf16[2,64,2048]{2,1,0:T(8,128)(2,1)}, u32[]{:S(2)}, u32[]{:S(2)}) collective-permute-start(bf16[2,64,2048]{2,1,0:T(8,128)(2,1)} %bitcast.255), channel_id=1, source_target_pairs={{0,4},{4,0},{8,12},{12,8},{16,20},{20,16},{24,28},{28,24},{1,5},{5... | collective-permute-start | bytes 1572872 | tf_op jit(solution)/shard_map/ppermute | solution.py:34
  247.2 9.2 %collective-permute-done.20 = bf16[1,1024,768]{2,1,0:T(8,128)(2,1)} collective-permute-done((bf16[1,1024,768]{2,1,0:T(8,128)(2,1)}, bf16[1,1024,768]{2,1,0:T(8,128)(2,1)}, u32[]{:S(2)}, u32[]{:S(2)}) %collective-permute-start.20) | collective-permute-done | bytes 1572896 | tf_op jit(solution)/shard_map/ppermute | solution.py:43
  261.6 13.2 %attend_back.3 = (bf16[64,2048]{1,0:T(8,128)(2,1)}, f32[2,64,2048]{2,1,0:T(8,128)}, bf16[1,2,64,2048]{3,2,1,0:T(8,128)(2,1)}) custom-call(s32[18]{0:T(128)} %pad_add_fusion.2.meta, bf16[3,3,64,512]{3,2,1,0:T(8,128)(2,1)} %bitcast.213, bf16[3,3,64,512]{3,2,1,0:T(8,128)(2,1)} %bitcast.217, bf16[3,3,64,512]{3,2,1,0:T(8,128)(2,1)} %bitcast.221, ...), custom_call_target="tpu_custom_call" | custom-call | flops 15000000512 | bytes 20000000 | tf_op jit(solution)/shard_map/attend_back/pallas_call | solution.py:337
  288.6 13.4 %attend_back.4 = (bf16[64,2048]{1,0:T(8,128)(2,1)}, f32[2,64,2048]{2,1,0:T(8,128)}, bf16[1,2,64,2048]{3,2,1,0:T(8,128)(2,1)}) custom-call(s32[18]{0:T(128)} %pad_add_fusion.2.meta, bf16[3,3,64,512]{3,2,1,0:T(8,128)(2,1)} %bitcast.214, bf16[3,3,64,512]{3,2,1,0:T(8,128)(2,1)} %bitcast.218, bf16[3,3,64,512]{3,2,1,0:T(8,128)(2,1)} %bitcast.222, ...), custom_call_target="tpu_custom_call" | custom-call | flops 15000000512 | bytes 20000000 | tf_op jit(solution)/shard_map/attend_back/pallas_call | solution.py:337
  302.1 7.6 %collective-permute-start.35 = (bf16[192,2304]{1,0:T(8,128)(2,1)S(1)}, bf16[192,2304]{1,0:T(8,128)(2,1)S(1)}, u32[]{:S(2)}, u32[]{:S(2)}) collective-permute-start(bf16[192,2304]{1,0:T(8,128)(2,1)S(1)} %copy-done.1), channel_id=1, source_target_pairs={{0,2},{1,3},{2,0},{3,1},{4,6},{5,7},{6,4},{7,5},{8,10},{9,11},{10,... | collective-permute-start | bytes 2654216 | tf_op jit(solution)/shard_map/ppermute | solution.py:43
  317.9 5.2 %collective-permute-done.34 = bf16[2,64,2048]{2,1,0:T(8,128)(2,1)S(1)} collective-permute-done((bf16[2,64,2048]{2,1,0:T(8,128)(2,1)S(1)}, bf16[2,64,2048]{2,1,0:T(8,128)(2,1)S(1)}, u32[]{:S(2)}, u32[]{:S(2)}) %collective-permute-start.34) | collective-permute-done | bytes 524320 | tf_op jit(solution)/shard_map/ppermute | solution.py:34
  329.1 7.6 %qkv_grads.1 = (bf16[2,208,576]{2,1,0:T(8,128)(2,1)}, bf16[2,208,576]{2,1,0:T(8,128)(2,1)}) custom-call(s32[2]{0:T(128)} %pad_add_fusion.3.which, bf16[512,768]{1,0:T(8,128)(2,1)} %bitcast.253, bf16[512,768]{1,0:T(8,128)(2,1)} %collective-permute-done.7.refs_1_, bf16[512,768]{1,0:T(8,128)(2,1)} %collective-permute-done.8.refs_2_, ...), custom_call_target="tpu_custom_call" | custom-call | flops 1811939328 | bytes 8000000 | tf_op jit(solution)/shard_map/qkv_grads/pallas_call | solution.py:581
  336.7 7.6 %collective-permute-done.37 = bf16[3,64,512]{2,1,0:T(8,128)(2,1)S(1)} collective-permute-done((bf16[3,64,512]{2,1,0:T(8,128)(2,1)}, bf16[3,64,512]{2,1,0:T(8,128)(2,1)S(1)}, u32[]{:S(2)}, u32[]{:S(2)}) %collective-permute-start.37) | collective-permute-done | bytes 196640 | tf_op jit(solution)/shard_map/ppermute | solution.py:26
  344.3 5.2 %collective-permute-done.38 = bf16[3,64,512]{2,1,0:T(8,128)(2,1)S(1)} collective-permute-done((bf16[3,64,512]{2,1,0:T(8,128)(2,1)}, bf16[3,64,512]{2,1,0:T(8,128)(2,1)S(1)}, u32[]{:S(2)}, u32[]{:S(2)}) %collective-permute-start.38) | collective-permute-done | bytes 196640 | tf_op jit(solution)/shard_map/ppermute | solution.py:26
  349.5 11.8 %collective-permute-done.33 = bf16[448,768]{1,0:T(8,128)(2,1)} collective-permute-done((bf16[448,768]{1,0:T(8,128)(2,1)}, bf16[448,768]{1,0:T(8,128)(2,1)}, u32[]{:S(2)}, u32[]{:S(2)}) %collective-permute-start.33) | collective-permute-done | bytes 688160 | tf_op jit(solution)/shard_map/ppermute | solution.py:43
  371.0 12.0 %collective-permute-done.41 = bf16[448,768]{1,0:T(8,128)(2,1)} collective-permute-done((bf16[448,768]{1,0:T(8,128)(2,1)S(1)}, bf16[448,768]{1,0:T(8,128)(2,1)}, u32[]{:S(2)}, u32[]{:S(2)}) %collective-permute-start.41) | collective-permute-done | bytes 688160 | tf_op jit(solution)/shard_map/ppermute | solution.py:43
  386.1 4.1 maximum_select_fusion.2
  403.9 4.2 collective-permute-done.48
  411.6 14.0 %collective-permute-done.49 = bf16[208,576]{1,0:T(8,128)(2,1)S(1)} collective-permute-done((bf16[208,576]{1,0:T(8,128)(2,1)S(1)}, bf16[208,576]{1,0:T(8,128)(2,1)S(1)}, u32[]{:S(2)}, u32[]{:S(2)}) %collective-permute-start.49) | collective-permute-done | bytes 239648 | tf_op jit(solution)/shard_map/ppermute | solution.py:26
  426.5 8.3 %collective-permute-done.50 = bf16[208,576]{1,0:T(8,128)(2,1)S(1)} collective-permute-done((bf16[208,576]{1,0:T(8,128)(2,1)S(1)}, bf16[208,576]{1,0:T(8,128)(2,1)S(1)}, u32[]{:S(2)}, u32[]{:S(2)}) %collective-permute-start.50) | collective-permute-done | bytes 239648 | tf_op jit(solution)/shard_map/ppermute | solution.py:26
  438.8 3.9 slice.199
  (358 shorter events, 202.2 us)
Async XLA Ops:
  0.6 60.2 %collective-permute-start.7 = (bf16[512,768]{1,0:T(8,128)(2,1)}, bf16[512,768]{1,0:T(8,128)(2,1)}, u32[]{:S(2)}, u32[]{:S(2)}) collective-permute-start(bf16[512,768]{1,0:T(8,128)(2,1)} %bitcast.249), channel_id=1, source_target_pairs={{0,8},{4,12},{8,0},{12,4},{16,24},{20,28},{24,16},{28,20},{1,9},{5... | collective-permute-start | bytes 2359304 | tf_op jit(solution)/shard_map/ppermute | solution.py:26
  0.7 62.1 %collective-permute-start.8 = (bf16[512,768]{1,0:T(8,128)(2,1)}, bf16[512,768]{1,0:T(8,128)(2,1)}, u32[]{:S(2)}, u32[]{:S(2)}) collective-permute-start(bf16[512,768]{1,0:T(8,128)(2,1)} %bitcast.250), channel_id=1, source_target_pairs={{0,16},{4,20},{8,24},{12,28},{16,0},{20,4},{24,8},{28,12},{1,17},{... | collective-permute-start | bytes 2359304 | tf_op jit(solution)/shard_map/ppermute | solution.py:26
  3.8 68.4 %collective-permute-start.9 = (bf16[512,768]{1,0:T(8,128)(2,1)}, bf16[512,768]{1,0:T(8,128)(2,1)}, u32[]{:S(2)}, u32[]{:S(2)}) collective-permute-start(bf16[512,768]{1,0:T(8,128)(2,1)} %bitcast.251), channel_id=1, source_target_pairs={{0,24},{4,28},{8,16},{12,20},{16,8},{20,12},{24,0},{28,4},{1,25},{... | collective-permute-start | bytes 2359304 | tf_op jit(solution)/shard_map/ppermute | solution.py:26
  18.2 28.6 %collective-permute-start.3 = (bf16[192,3072]{1,0:T(8,128)(2,1)S(1)}, bf16[192,3072]{1,0:T(8,128)(2,1)S(1)}, u32[]{:S(2)}, u32[]{:S(2)}) collective-permute-start(bf16[192,3072]{1,0:T(8,128)(2,1)S(1)} %copy-done.5), channel_id=1, source_target_pairs={{0,2},{1,3},{2,0},{3,1},{4,6},{5,7},{6,4},{7,5},{8,10},{9,11},{10,... | collective-permute-start | bytes 3538952 | tf_op jit(solution)/shard_map/ppermute | solution.py:43
  48.5 36.3 %collective-permute-start.6 = (bf16[2,192,3072]{2,1,0:T(8,128)(2,1)}, bf16[2,192,3072]{2,1,0:T(8,128)(2,1)}, u32[]{:S(2)}, u32[]{:S(2)}) collective-permute-start(bf16[2,192,3072]{2,1,0:T(8,128)(2,1)} %maximum_select_fusion.4), channel_id=1, source_target_pairs={{0,1},{1,0},{2,3},{3,2},{4,5},{5,4},{6,7},{7,6},{8,9},{9,8},{10,11... | collective-permute-start | bytes 7077896 | tf_op jit(solution)/shard_map/ppermute | solution.py:43
  53.0 27.3 %collective-permute-start.16 = (bf16[768,768]{1,0:T(8,128)(2,1)S(1)}, bf16[768,768]{1,0:T(8,128)(2,1)S(1)}, u32[]{:S(2)}, u32[]{:S(2)}) collective-permute-start(bf16[768,768]{1,0:T(8,128)(2,1)S(1)} %copy-done.4), channel_id=1, source_target_pairs={{0,2},{1,3},{2,0},{3,1},{4,6},{5,7},{6,4},{7,5},{8,10},{9,11},{10,... | collective-permute-start | bytes 3538952 | tf_op jit(solution)/shard_map/ppermute | solution.py:43
  62.8 28.2 %collective-permute-start.10 = (bf16[2,3,64,512]{3,2,1,0:T(8,128)(2,1)S(1)}, bf16[2,3,64,512]{3,2,1,0:T(8,128)(2,1)S(1)}, u32[]{:S(2)}, u32[]{:S(2)}) collective-permute-start(bf16[2,3,64,512]{3,2,1,0:T(8,128)(2,1)S(1)} %bitcast.204), channel_id=1, source_target_pairs={{0,4},{4,0},{8,12},{12,8},{16,20},{20,16},{24,28},{28,24},{1,5},{5... | collective-permute-start | bytes 1179656 | tf_op jit(solution)/shard_map/ppermute | solution.py:34
  82.1 42.3 %collective-permute-start.17 = (bf16[2,768,768]{2,1,0:T(8,128)(2,1)}, bf16[2,768,768]{2,1,0:T(8,128)(2,1)}, u32[]{:S(2)}, u32[]{:S(2)}) collective-permute-start(bf16[2,768,768]{2,1,0:T(8,128)(2,1)} %maximum_select_fusion.6), channel_id=1, source_target_pairs={{0,1},{1,0},{2,3},{3,2},{4,5},{5,4},{6,7},{7,6},{8,9},{9,8},{10,11... | collective-permute-start | bytes 7077896 | tf_op jit(solution)/shard_map/ppermute | solution.py:43
  216.1 29.1 %collective-permute-start.21 = (bf16[2,192,1536]{2,1,0:T(8,128)(2,1)}, bf16[2,192,1536]{2,1,0:T(8,128)(2,1)}, u32[]{:S(2)}, u32[]{:S(2)}) collective-permute-start(bf16[2,192,1536]{2,1,0:T(8,128)(2,1)} %constant_dynamic-slice_fusion.10), channel_id=1, source_target_pairs={{0,4},{4,0},{8,12},{12,8},{16,20},{20,16},{24,28},{28,24},{1,5},{5... | collective-permute-start | bytes 3538952 | tf_op jit(solution)/shard_map/ppermute | solution.py:43
  219.9 36.5 %collective-permute-start.20 = (bf16[1,1024,768]{2,1,0:T(8,128)(2,1)}, bf16[1,1024,768]{2,1,0:T(8,128)(2,1)}, u32[]{:S(2)}, u32[]{:S(2)}) collective-permute-start(bf16[1,1024,768]{2,1,0:T(8,128)(2,1)} %constant_dynamic-slice_fusion.11), channel_id=1, source_target_pairs={{0,2},{1,3},{2,0},{3,1},{4,6},{5,7},{6,4},{7,5},{8,10},{9,11},{10,... | collective-permute-start | bytes 4718600 | tf_op jit(solution)/shard_map/ppermute | solution.py:43
  238.5 44.6 %collective-permute-start.29 = (bf16[2,64,2048]{2,1,0:T(8,128)(2,1)}, bf16[2,64,2048]{2,1,0:T(8,128)(2,1)}, u32[]{:S(2)}, u32[]{:S(2)}) collective-permute-start(bf16[2,64,2048]{2,1,0:T(8,128)(2,1)} %bitcast.255), channel_id=1, source_target_pairs={{0,4},{4,0},{8,12},{12,8},{16,20},{20,16},{24,28},{28,24},{1,5},{5... | collective-permute-start | bytes 1572872 | tf_op jit(solution)/shard_map/ppermute | solution.py:34
  279.6 32.3 %collective-permute-start.28 = (bf16[2,64,2048]{2,1,0:T(8,128)(2,1)}, bf16[2,64,2048]{2,1,0:T(8,128)(2,1)}, u32[]{:S(2)}, u32[]{:S(2)}) collective-permute-start(bf16[2,64,2048]{2,1,0:T(8,128)(2,1)} %bitcast.57), channel_id=1, source_target_pairs={{0,4},{4,0},{8,12},{12,8},{16,20},{20,16},{24,28},{28,24},{1,5},{5... | collective-permute-start | bytes 1572872 | tf_op jit(solution)/shard_map/ppermute | solution.py:34
  285.1 28.9 %collective-permute-start.30 = (bf16[3,64,512]{2,1,0:T(8,128)(2,1)}, bf16[3,64,512]{2,1,0:T(8,128)(2,1)}, u32[]{:S(2)}, u32[]{:S(2)}) collective-permute-start(bf16[3,64,512]{2,1,0:T(8,128)(2,1)} %get-tuple-element.213), channel_id=1, source_target_pairs={{0,8},{4,12},{8,0},{12,4},{16,24},{20,28},{24,16},{28,20},{1,9},{5... | collective-permute-start | bytes 589832 | tf_op jit(solution)/shard_map/ppermute | solution.py:26
  286.4 29.9 %collective-permute-start.31 = (bf16[3,64,512]{2,1,0:T(8,128)(2,1)S(1)}, bf16[3,64,512]{2,1,0:T(8,128)(2,1)}, u32[]{:S(2)}, u32[]{:S(2)}) collective-permute-start(bf16[3,64,512]{2,1,0:T(8,128)(2,1)S(1)} %get-tuple-element.214), channel_id=1, source_target_pairs={{0,16},{4,20},{8,24},{12,28},{16,0},{20,4},{24,8},{28,12},{1,17},{... | collective-permute-start | bytes 589832 | tf_op jit(solution)/shard_map/ppermute | solution.py:26
  288.1 29.2 %collective-permute-start.32 = (bf16[3,64,512]{2,1,0:T(8,128)(2,1)S(1)}, bf16[3,64,512]{2,1,0:T(8,128)(2,1)}, u32[]{:S(2)}, u32[]{:S(2)}) collective-permute-start(bf16[3,64,512]{2,1,0:T(8,128)(2,1)S(1)} %get-tuple-element.211), channel_id=1, source_target_pairs={{0,24},{4,28},{8,16},{12,20},{16,8},{20,12},{24,0},{28,4},{1,25},{... | collective-permute-start | bytes 589832 | tf_op jit(solution)/shard_map/ppermute | solution.py:26
  302.1 47.4 %collective-permute-start.35 = (bf16[192,2304]{1,0:T(8,128)(2,1)S(1)}, bf16[192,2304]{1,0:T(8,128)(2,1)S(1)}, u32[]{:S(2)}, u32[]{:S(2)}) collective-permute-start(bf16[192,2304]{1,0:T(8,128)(2,1)S(1)} %copy-done.1), channel_id=1, source_target_pairs={{0,2},{1,3},{2,0},{3,1},{4,6},{5,7},{6,4},{7,5},{8,10},{9,11},{10,... | collective-permute-start | bytes 2654216 | tf_op jit(solution)/shard_map/ppermute | solution.py:43
  316.2 28.0 %collective-permute-start.37 = (bf16[3,64,512]{2,1,0:T(8,128)(2,1)}, bf16[3,64,512]{2,1,0:T(8,128)(2,1)S(1)}, u32[]{:S(2)}, u32[]{:S(2)}) collective-permute-start(bf16[3,64,512]{2,1,0:T(8,128)(2,1)} %get-tuple-element.210), channel_id=1, source_target_pairs={{0,16},{4,20},{8,24},{12,28},{16,0},{20,4},{24,8},{28,12},{1,17},{... | collective-permute-start | bytes 589832 | tf_op jit(solution)/shard_map/ppermute | solution.py:26
  317.3 32.3 %collective-permute-start.38 = (bf16[3,64,512]{2,1,0:T(8,128)(2,1)}, bf16[3,64,512]{2,1,0:T(8,128)(2,1)S(1)}, u32[]{:S(2)}, u32[]{:S(2)}) collective-permute-start(bf16[3,64,512]{2,1,0:T(8,128)(2,1)} %get-tuple-element.207), channel_id=1, source_target_pairs={{0,24},{4,28},{8,16},{12,20},{16,8},{20,12},{24,0},{28,4},{1,25},{... | collective-permute-start | bytes 589832 | tf_op jit(solution)/shard_map/ppermute | solution.py:26
  323.1 38.2 %collective-permute-start.33 = (bf16[448,768]{1,0:T(8,128)(2,1)}, bf16[448,768]{1,0:T(8,128)(2,1)}, u32[]{:S(2)}, u32[]{:S(2)}) collective-permute-start(bf16[448,768]{1,0:T(8,128)(2,1)} %add_convert_fusion.6), channel_id=1, source_target_pairs={{0,16},{4,20},{8,24},{12,28},{16,0},{20,4},{24,8},{28,12},{1,17},{... | collective-permute-start | bytes 2064392 | tf_op jit(solution)/shard_map/ppermute | solution.py:43
  392.8 51.1 %collective-permute-start.44 = (bf16[3,64,512]{2,1,0:T(8,128)(2,1)}, bf16[3,64,512]{2,1,0:T(8,128)(2,1)}, u32[]{:S(2)}, u32[]{:S(2)}) collective-permute-start(bf16[3,64,512]{2,1,0:T(8,128)(2,1)} %get-tuple-element.203), channel_id=1, source_target_pairs={{0,8},{4,12},{8,0},{12,4},{16,24},{20,28},{24,16},{28,20},{1,9},{5... | collective-permute-start | bytes 589832 | tf_op jit(solution)/shard_map/ppermute | solution.py:26
  394.6 49.4 %collective-permute-start.43 = (bf16[896,768]{1,0:T(8,128)(2,1)}, bf16[896,768]{1,0:T(8,128)(2,1)}, u32[]{:S(2)}, u32[]{:S(2)}) collective-permute-start(bf16[896,768]{1,0:T(8,128)(2,1)} %maximum_select_fusion.10), channel_id=1, source_target_pairs={{0,4},{4,0},{8,12},{12,8},{16,20},{20,16},{24,28},{28,24},{1,5},{5... | collective-permute-start | bytes 4128776 | tf_op jit(solution)/shard_map/ppermute | solution.py:43
  399.7 25.9 %collective-permute-start.49 = (bf16[208,576]{1,0:T(8,128)(2,1)S(1)}, bf16[208,576]{1,0:T(8,128)(2,1)S(1)}, u32[]{:S(2)}, u32[]{:S(2)}) collective-permute-start(bf16[208,576]{1,0:T(8,128)(2,1)S(1)} %fusion.8), channel_id=1, source_target_pairs={{0,16},{4,20},{8,24},{12,28},{16,0},{20,4},{24,8},{28,12},{1,17},{... | collective-permute-start | bytes 718856 | tf_op jit(solution)/shard_map/ppermute | solution.py:26
  401.5 33.3 %collective-permute-start.50 = (bf16[208,576]{1,0:T(8,128)(2,1)S(1)}, bf16[208,576]{1,0:T(8,128)(2,1)S(1)}, u32[]{:S(2)}, u32[]{:S(2)}) collective-permute-start(bf16[208,576]{1,0:T(8,128)(2,1)S(1)} %fusion.8), channel_id=1, source_target_pairs={{0,24},{4,28},{8,16},{12,20},{16,8},{20,12},{24,0},{28,4},{1,25},{... | collective-permute-start | bytes 718856 | tf_op jit(solution)/shard_map/ppermute | solution.py:26
  408.1 35.8 %collective-permute-start.45 = (bf16[3,64,512]{2,1,0:T(8,128)(2,1)}, bf16[3,64,512]{2,1,0:T(8,128)(2,1)}, u32[]{:S(2)}, u32[]{:S(2)}) collective-permute-start(bf16[3,64,512]{2,1,0:T(8,128)(2,1)} %get-tuple-element.202), channel_id=1, source_target_pairs={{0,16},{4,20},{8,24},{12,28},{16,0},{20,4},{24,8},{28,12},{1,17},{... | collective-permute-start | bytes 589832 | tf_op jit(solution)/shard_map/ppermute | solution.py:26
  (90 other events, 700.6 us)

commit v2 on v1

--- a/solution.py
+++ b/solution.py
@@ -245,11 +245,11 @@
 
     lax.fori_loop(0, groups, one_slot, 0)
     g, s = meta[0], meta[1]
-    for j in range(groups):
+
+    def finish(j, carry):
+        at = pl.ds(pl.multiple_of(j * rows, rows), rows)
         for e in range(parts):
-            block = (g ^ j) * parts + lax.rem(s - e + parts, parts)
-            terms = accum_ref[block].T
-            at = slice(j * rows, (j + 1) * rows)
+            terms = accum_ref[(g ^ j) * parts + lax.rem(s - e + parts, parts)].T
             d_key = terms[:HD] * HD**-0.5
             d_value = terms[HD:]
             if e == 0:
@@ -258,6 +258,9 @@
             else:
                 theirs[e - 1, 0, :, at] = d_key.astype(jnp.bfloat16)
                 theirs[e - 1, 1, :, at] = d_value.astype(jnp.bfloat16)
+        return carry
+
+    lax.fori_loop(0, groups, finish, 0)
 
 
 def head_block(head, *shape):
@@ -415,8 +418,16 @@
         in_sums_ref[...] = jnp.zeros_like(in_sums_ref)
 
     total = lambda a: jnp.sum(a, axis=0, keepdims=True)
-    branch = dot(attended_ref[...].T, out_ref[...]) + out_shift
-    unit1, scale1 = normed(tokens_ref[...].astype(f32) + branch)
+    width = out_ref.shape[0]
+    step = math.gcd(width, 256)
+    part = lambda i: pl.ds(pl.multiple_of(i * step, step), step)
+    resid1 = lax.fori_loop(
+        0,
+        width // step,
+        lambda i, value: value + dot(attended_ref[part(i), :].T, out_ref[part(i), :]),
+        tokens_ref[...].astype(f32) + out_shift,
+    )
+    unit1, scale1 = normed(resid1)
     hidden = unit1 * gain_one + shift_one
     hidden_low = hidden.astype(bf16)
     count, unused, shard = hidden_ref.shape
@@ -424,19 +435,21 @@
         hidden_ref[i] = hidden_low[:, i * shard : (i + 1) * shard]
     resid2 = hidden + back_shift
     blocks, unused, size = act_ref.shape
-    aligned = size % 128 == 0
-    columns = lambda i: pl.ds(pl.multiple_of(i * size, size) if aligned else i * size, size)
+    pieces = size // 256 if size % 256 == 0 else 1
+    piece = size // pieces
+    aligned = piece % 128 == 0
+    columns = lambda i: pl.ds(pl.multiple_of(i * piece, piece) if aligned else i * piece, piece)
 
     def forward(i, resid2):
         cols = columns(i)
         pre = dot(hidden_low, in_ref[:, cols]) + in_bias_ref[:, cols]
         below, density = normal_terms(pre)
         act = (pre * below).astype(bf16)
-        act_ref[i] = act
+        act_ref[i // pieces, :, columns(i % pieces)] = act
         slope_ref[i] = below + pre * density
         return resid2 + dot(act, back_ref[cols, :])
 
-    resid2 = over_blocks(blocks, aligned, forward, hidden + back_shift)
+    resid2 = over_blocks(blocks * pieces, aligned, forward, hidden + back_shift)
     unit2, scale2 = normed(resid2)
     result_ref[...] = (unit2 * gain_two + shift_two).astype(bf16)
     cot = cot_ref[...].astype(f32)
@@ -452,12 +465,17 @@
         in_sums_ref[:, cols] += total(d_pre.astype(f32))
         return d_hidden + dot_t(d_pre, in_ref[:, cols])
 
-    d_hidden = over_blocks(blocks, aligned, backward, d_resid2)
+    d_hidden = over_blocks(blocks * pieces, aligned, backward, d_resid2)
     d_resid1 = norm_back(d_hidden, gain_one, unit1, scale1)
     d_resid1_ref[...] = d_resid1
     d_branch = d_resid1.astype(bf16)
     d_branch_ref[...] = d_branch
-    d_attended_ref[...] = dot_t(out_ref[...], d_branch).astype(bf16)
+
+    def attended_step(i, carry):
+        d_attended_ref[part(i), :] = dot_t(out_ref[part(i), :], d_branch).astype(bf16)
+        return carry
+
+    lax.fori_loop(0, width // step, attended_step, 0)
     sums_ref[...] += jnp.concatenate(
         [
             total(d_branch.astype(f32)),
@@ -477,6 +495,7 @@
     rows, model = tokens.shape
     inner = in_full.shape[1]
     tile = math.gcd(rows, 256)
+    pieces = inner // fsdp // 256 if (inner // fsdp) % 256 == 0 else 1
     by_rows = lambda n: pl.BlockSpec((tile, n), lambda i: (i, 0))
     by_cols = lambda n: pl.BlockSpec((n, tile), lambda i: (0, i))
     blocks = lambda n: pl.BlockSpec((fsdp, tile, n // fsdp), lambda i: (0, i, 0))
@@ -500,7 +519,7 @@
             shape((rows, inner), bf16), shape((rows, model), bf16), shape((8, model), f32),
             shape((1, inner), f32),
         ],
-        scratch_shapes=[pltpu.VMEM((fsdp, tile, inner // fsdp), f32)],
+        scratch_shapes=[pltpu.VMEM((fsdp * pieces, tile, inner // (fsdp * pieces)), f32)],
         cost_estimate=pl.CostEstimate(
             flops=rows * model * (8 * inner + 4 * model), transcendentals=0, bytes_accessed=30_000_000
         ),
@@ -511,14 +530,29 @@
 def weight_grad_kernel(which, *refs):
     ins, (d_ffn, d_pre, d_branch), outs = refs[:8], refs[8:11], refs[11:]
     bf16 = jnp.bfloat16
+    first, second = ins[0].shape[2], ins[2].shape[0]
+    size = math.gcd(first, 256)
+    wide = math.gcd(d_pre.shape[1], 768)
+    at = lambda i, n: pl.ds(i * n if isinstance(i, int) else pl.multiple_of(i * n, n), n)
+
+    def rows_step(i, carry):
+        for side in range(2):
+            outs[2 * side][0, at(i, size)] = dot(ins[4 * side][0, :, at(i, size)].T, d_ffn[...]).astype(bf16)
+        return carry
+
+    over_blocks(first // size, size % 128 == 0, rows_step, 0)
+    turned = [ins[4 * side + 1][0].T for side in range(2)]
+
+    def columns_step(i, carry):
+        for side in range(2):
+            outs[2 * side + 1][0, :, at(i, wide)] = dot(turned[side], d_pre[:, at(i, wide)]).astype(bf16)
+        return carry
+
+    over_blocks(d_pre.shape[1] // wide, True, columns_step, 0)
     for side in range(2):
-        act, hidden, attended_t, line = ins[4 * side : 4 * side + 4]
-        lower, upper = outs[2 * side : 2 * side + 2]
-        first, second = act.shape[2], attended_t.shape[0]
-        lower[0, :first] = dot(act[0].T, d_ffn[...]).astype(bf16)
-        lower[0, first : first + second] = dot(attended_t[...], d_branch[...]).astype(bf16)
-        lower[0, first + second :] = line[0].astype(bf16)
-        upper[0] = dot(hidden[0].T, d_pre[...]).astype(bf16)
+        lower = outs[2 * side]
+        lower[0, first : first + second] = dot(ins[4 * side + 2][...], d_branch[...]).astype(bf16)
+        lower[0, first + second :] = ins[4 * side + 3][0].astype(bf16)
 
 
 def weight_grads(which, act, hidden, attended_t, line, d_ffn, d_pre, d_branch):
@@ -559,11 +593,18 @@
     slots, (d_qkv, send, keep, total) = refs[:-4], refs[-4:]
     rows = slots[0].shape[0]
     shard = send.shape[1] - PAD
-    value = None
-    for j, slot in enumerate(slots):
-        term = dot_t(slot[...].T, d_qkv[:, j * rows : (j + 1) * rows])
-        value = term if value is None else value + term
-    total[...] = value
+    size = math.gcd(total.shape[0], 256)
+
+    def step(i, carry):
+        at = pl.ds(pl.multiple_of(i * size, size), size)
+        value = None
+        for j, slot in enumerate(slots):
+            term = dot_t(slot[:, at].T, d_qkv[:, j * rows : (j + 1) * rows])
+            value = term if value is None else value + term
+        total[at] = value
+        return carry
+
+    lax.fori_loop(0, total.shape[0] // size, step, 0)
     ones = jnp.ones((PAD, d_qkv.shape[1]), jnp.bfloat16)
     sums = dot_t(ones, d_qkv[...]).astype(jnp.bfloat16)
     for side, ref in enumerate((send, keep)):
@@ -632,7 +673,9 @@
 
     slots = gather_groups(tokens, groups, parts)
 
-    own_cols = pick(qkv_weight.reshape(shard, 3, groups, span), g, 2).reshape(shard, width)
+    own_cols = jnp.concatenate(
+        [lax.dynamic_slice_in_dim(qkv_weight, i * model + g * span, span, 1) for i in range(3)], axis=1
+    )
     small = jnp.concatenate(
         [
             query_bias, value_bias, out_bias, norm1_gain, norm1_bias,
@@ -818,11 +861,12 @@
     by_group = jnp.zeros((groups,) + qkv_low.shape, bf16)
     turns = [ctx_swap(qkv_low, groups, parts, j) if j else qkv_low for j in range(groups)]
     other, *late = together(other, *late)
-    turns = together(*turns)
+    turns = list(together(*turns))
     for j, piece in enumerate(turns):
         by_group = lax.dynamic_update_slice(by_group, piece[None], (g ^ j, 0, 0))
-    natural = by_group.reshape(groups, shard + PAD, 3, span).transpose(1, 2, 0, 3)
-    natural = natural.reshape(shard + PAD, 3 * model).astype(f32)
+    natural = jnp.concatenate(
+        [by_group[b, :, i * span : (i + 1) * span] for i in range(3) for b in range(groups)], axis=1
+    ).astype(f32)
     grad_qkv_shard = natural[:shard]
     bias_line = natural[shard]
     grad_query_shift = lax.dynamic_slice(bias_line, (f * shard,), (shard,))

time: 467 us -> 484 us (1.036)
  Pallas kernels: 121 us -> 180 us
  starting transfers between devices: 88.5 us -> 51.1 us
  local copies, waits for them, and re-layouts: 55.8 us -> 45 us
  waiting for transfers between devices: 118 us -> 125 us
    ppermute x22, starting transfers between devices: 44.4 us -> 17.1 us  [swap(): return lax.ppermute(array, axis, [(i, i ^ 1 << bit) for i in range(size)])]
    pallas_call x1, Pallas kernels: 34.6 us -> 55.4 us  [feed_forward(): pl.pallas_call(feed_kernel, grid=(rows // tile,), in_specs=[by_rows(model...]
    pallas_call x3, Pallas kernels: 39.8 us -> 58.5 us  [attend_back(): pl.pallas_call(partial(attend_back_kernel, groups, parts, docs, rows), gr...]
    pallas_call x1, Pallas kernels: 26.5 us -> 42.3 us  [attend(): pl.pallas_call(partial(attend_kernel, groups, parts, docs, rows), grid_sp...]
    ppermute x8, starting transfers between devices: 15.9 us -> 5.87 us  [part_shift(): return lax.ppermute(array, 'ctx', pairs)]
    ppermute x22, waiting for transfers between devices: 51.1 us -> 59.2 us  [swap(): return lax.ppermute(array, axis, [(i, i ^ 1 << bit) for i in range(size)])]
    concatenate x1, local copies, waits for them, and re-layouts: 0.09 us -> 6.2 us  [body(): jnp.concatenate([query_bias, value_bias, out_bias, norm1_gain, norm1_bias...]
    slice x2 -> x1, local copies, waits for them, and re-layouts: 6.43 us -> 1.32 us  [body(): grad_qkv_shard = natural[:shard]]
  transfers between devices with their start and end apart: 51 -> 51, of which waited for: 22 -> 24; matrix products, arithmetic and copies ran while one was open for 21% -> 18% of each run, Pallas kernels for 16% -> 23%
where the time goes in v2:
time: 484 us; the launch traced here: 477 us
  Pallas kernels  180 us (37%)
  waiting for transfers between devices  125 us (26%)
  other arithmetic  63.5 us (13%)
  starting transfers between devices  51.1 us (11%)
  local copies, waits for them, and re-layouts  45 us (9%)
  matrix products  11 us (2%)
    ppermute x22, waiting for transfers between devices, swap(): return lax.ppermute(array, axis, [(i, i ^ 1 << bit) for i in range(size)])  59.2 us
    pallas_call x3, Pallas kernels, attend_back(): pl.pallas_call(partial(attend_back_kernel, groups, parts, docs, rows), gr...  58.5 us
    pallas_call x1, Pallas kernels, feed_forward(): pl.pallas_call(feed_kernel, grid=(rows // tile,), in_specs=[by_rows(model...  55.4 us
    ppermute x21, waiting for transfers between devices, ctx_swap(): return lax.ppermute(array, 'ctx', pairs)  53.8 us
    pallas_call x1, Pallas kernels, attend(): pl.pallas_call(partial(attend_kernel, groups, parts, docs, rows), grid_sp...  42.3 us
    select_n x17, other arithmetic, join(): jnp.where(mine == 0, jnp.concatenate([own, other], axis=dim), jnp.concate...  28.6 us
    ppermute x21, starting transfers between devices, ctx_swap(): return lax.ppermute(array, 'ctx', pairs)  28.1 us
    ppermute x22, starting transfers between devices, swap(): return lax.ppermute(array, axis, [(i, i ^ 1 << bit) for i in range(size)])  17.1 us
  transfers between devices with their start and end apart: 51, of which 24 were waited for; matrix products, arithmetic and copies ran while one was open for 18% of the time, Pallas kernels for 23%

profile of v2, /device:TPU:8, one launch (start us, length us, event | category | flops | bytes accessed | tf_op | source)
XLA Modules:
  0.0 477.4 jit_solution(5689741594203320142)
XLA Ops:
  4.2 6.2 %concatenate.232 = bf16[2304]{0:T(1024)(128)(2,1)S(1)} concatenate(bf16[192]{0:T(256)(128)(2,1)} %param.19, bf16[192]{0:T(256)(128)(2,1)} %param.20, bf16[192]{0:T(256)(128)(2,1)} %param.22, bf16[192]{0:T(256)(128)(2,1)} %param.23, bf16[192]{0:T(256)(128)(2,1)} %param.24, bf16[192]{0:T(256)(128)(2,1)} %param.28, bf16[192]{0:T(256)(128)(2,1)} %param.29, bf16[192]{0:T(256)(128)(2,1)} %param.30, ...), dimensions={0} | concatenate | bytes 9216 | tf_op jit(solution)/shard_map/concatenate | solution.py:679
  15.1 4.1 collective-permute-done
  32.9 8.9 %collective-permute-done.5.refs_4_ = bf16[2,3,64,512]{3,2,1,0:T(8,128)(2,1)S(1)} collective-permute-done((bf16[2,3,64,512]{3,2,1,0:T(8,128)(2,1)S(1)}, bf16[2,3,64,512]{3,2,1,0:T(8,128)(2,1)S(1)}, u32[]{:S(2)}, u32[]{:S(2)}) %collective-permute-start.5) | collective-permute-done | bytes 393248 | tf_op jit(solution)/shard_map/ppermute | solution.py:34
  43.3 6.1 %collective-permute-done.3 = bf16[192,3072]{1,0:T(8,128)(2,1)S(1)} collective-permute-done((bf16[192,3072]{1,0:T(8,128)(2,1)S(1)}, bf16[192,3072]{1,0:T(8,128)(2,1)S(1)}, u32[]{:S(2)}, u32[]{:S(2)}) %collective-permute-start.3) | collective-permute-done | bytes 1179680 | tf_op jit(solution)/shard_map/ppermute | solution.py:43
  51.8 3.6 collective-permute-done.1
  77.5 5.4 %collective-permute-done.16 = bf16[768,768]{1,0:T(8,128)(2,1)S(1)} collective-permute-done((bf16[768,768]{1,0:T(8,128)(2,1)S(1)}, bf16[768,768]{1,0:T(8,128)(2,1)S(1)}, u32[]{:S(2)}, u32[]{:S(2)}) %collective-permute-start.16) | collective-permute-done | bytes 1179680 | tf_op jit(solution)/shard_map/ppermute | solution.py:43
  94.8 42.3 %attend.1 = (bf16[3,64,2048]{2,1,0:T(8,128)(2,1)}, f32[3,64,2048]{2,1,0:T(8,128)}, f32[3,1,2048]{2,1,0:T(1,128)}) custom-call(s32[18]{0:T(128)} %pad_add_fusion.2.meta, bf16[3,3,64,512]{3,2,1,0:T(8,128)(2,1)} %bitcast.225, bf16[3,3,64,512]{3,2,1,0:T(8,128)(2,1)} %bitcast.229, bf16[3,3,64,512]{3,2,1,0:T(8,128)(2,1)} %bitcast.233, ...), custom_call_target="tpu_custom_call" | custom-call | flops 17999998976 | bytes 60000000 | tf_op jit(solution)/shard_map/attend/pallas_call | solution.py:293
  153.6 55.4 %feed_forward.1 = (bf16[512,768]{1,0:T(8,128)(2,1)}, f32[512,768]{1,0:T(8,128)}, bf16[768,512]{1,0:T(8,128)(2,1)}, bf16[4,512,192]{2,1,0:T(8,128)(2,1)}, bf16[4,...) custom-call(bf16[512,768]{1,0:T(8,128)(2,1)} %bitcast.266, ...), custom_call_target="tpu_custom_call" | custom-call | flops 10871635968 | bytes 30000000 | tf_op jit(solution)/shard_map/feed_forward/pallas_call | solution.py:504
  212.9 15.5 %weight_grads.1 = (bf16[2,1024,768]{2,1,0:T(8,128)(2,1)}, bf16[2,192,3072]{2,1,0:T(8,128)(2,1)}, bf16[2,1024,768]{2,1,0:T(8,128)(2,1)}, bf16[2,192,3072]{2,1,0:T(8,128)(2,1)}) custom-call(s32[2]{0:T(128)} %pad_add_fusion.3.which, bf16[4,512,768]{2,1,0:T(8,128)(2,1)} %get-tuple-element.121.refs_0_.refs_4_, ...), custom_call_target="tpu_custom_call" | custom-call | flops 5435817984 | bytes 25000000 | tf_op jit(solution)/shard_map/weight_grads/pallas_call | solution.py:576
  246.6 4.0 collective-permute-done.24.refs_11_
  251.2 19.6 %attend_back.5 = (bf16[64,2048]{1,0:T(8,128)(2,1)}, f32[2,64,2048]{2,1,0:T(8,128)}, bf16[1,2,64,2048]{3,2,1,0:T(8,128)(2,1)}) custom-call(s32[18]{0:T(128)} %pad_add_fusion.2.meta, bf16[3,3,64,512]{3,2,1,0:T(8,128)(2,1)} %bitcast.226, bf16[3,3,64,512]{3,2,1,0:T(8,128)(2,1)} %bitcast.230, bf16[3,3,64,512]{3,2,1,0:T(8,128)(2,1)} %bitcast.234, ...), custom_call_target="tpu_custom_call" | custom-call | flops 15000000512 | bytes 20000000 | tf_op jit(solution)/shard_map/attend_back/pallas_call | solution.py:340
  272.9 8.2 %collective-permute-done.20 = bf16[1,1024,768]{2,1,0:T(8,128)(2,1)} collective-permute-done((bf16[1,1024,768]{2,1,0:T(8,128)(2,1)}, bf16[1,1024,768]{2,1,0:T(8,128)(2,1)}, u32[]{:S(2)}, u32[]{:S(2)}) %collective-permute-start.20) | collective-permute-done | bytes 1572896 | tf_op jit(solution)/shard_map/ppermute | solution.py:43
  285.0 19.5 %attend_back.3 = (bf16[64,2048]{1,0:T(8,128)(2,1)}, f32[2,64,2048]{2,1,0:T(8,128)}, bf16[1,2,64,2048]{3,2,1,0:T(8,128)(2,1)}) custom-call(s32[18]{0:T(128)} %pad_add_fusion.2.meta, bf16[3,3,64,512]{3,2,1,0:T(8,128)(2,1)} %bitcast.227, bf16[3,3,64,512]{3,2,1,0:T(8,128)(2,1)} %bitcast.231, bf16[3,3,64,512]{3,2,1,0:T(8,128)(2,1)} %bitcast.235, ...), custom_call_target="tpu_custom_call" | custom-call | flops 15000000512 | bytes 20000000 | tf_op jit(solution)/shard_map/attend_back/pallas_call | solution.py:340
  313.3 19.4 %attend_back.4 = (bf16[64,2048]{1,0:T(8,128)(2,1)}, f32[2,64,2048]{2,1,0:T(8,128)}, bf16[1,2,64,2048]{3,2,1,0:T(8,128)(2,1)}) custom-call(s32[18]{0:T(128)} %pad_add_fusion.2.meta, bf16[3,3,64,512]{3,2,1,0:T(8,128)(2,1)} %bitcast.228, bf16[3,3,64,512]{3,2,1,0:T(8,128)(2,1)} %bitcast.232, bf16[3,3,64,512]{3,2,1,0:T(8,128)(2,1)} %bitcast.236, ...), custom_call_target="tpu_custom_call" | custom-call | flops 15000000512 | bytes 20000000 | tf_op jit(solution)/shard_map/attend_back/pallas_call | solution.py:340
  349.9 8.1 %qkv_grads.1 = (bf16[2,208,576]{2,1,0:T(8,128)(2,1)}, bf16[2,208,576]{2,1,0:T(8,128)(2,1)}) custom-call(s32[2]{0:T(128)} %pad_add_fusion.3.which, bf16[512,768]{1,0:T(8,128)(2,1)} %bitcast.267, bf16[512,768]{1,0:T(8,128)(2,1)} %collective-permute-done.7.refs_1_, bf16[512,768]{1,0:T(8,128)(2,1)} %collective-permute-done.8.refs_2_, ...), custom_call_target="tpu_custom_call" | custom-call | flops 1811939328 | bytes 8000000 | tf_op jit(solution)/shard_map/qkv_grads/pallas_call | solution.py:622
  358.0 6.5 %collective-permute-done.37 = bf16[3,64,512]{2,1,0:T(8,128)(2,1)S(1)} collective-permute-done((bf16[3,64,512]{2,1,0:T(8,128)(2,1)}, bf16[3,64,512]{2,1,0:T(8,128)(2,1)S(1)}, u32[]{:S(2)}, u32[]{:S(2)}) %collective-permute-start.37) | collective-permute-done | bytes 196640 | tf_op jit(solution)/shard_map/ppermute | solution.py:26
  364.5 5.2 %collective-permute-done.38 = bf16[3,64,512]{2,1,0:T(8,128)(2,1)S(1)} collective-permute-done((bf16[3,64,512]{2,1,0:T(8,128)(2,1)}, bf16[3,64,512]{2,1,0:T(8,128)(2,1)S(1)}, u32[]{:S(2)}, u32[]{:S(2)}) %collective-permute-start.38) | collective-permute-done | bytes 196640 | tf_op jit(solution)/shard_map/ppermute | solution.py:26
  369.7 11.8 %collective-permute-done.33 = bf16[448,768]{1,0:T(8,128)(2,1)} collective-permute-done((bf16[448,768]{1,0:T(8,128)(2,1)}, bf16[448,768]{1,0:T(8,128)(2,1)}, u32[]{:S(2)}, u32[]{:S(2)}) %collective-permute-start.33) | collective-permute-done | bytes 688160 | tf_op jit(solution)/shard_map/ppermute | solution.py:43
  390.1 14.2 %collective-permute-done.41 = bf16[448,768]{1,0:T(8,128)(2,1)} collective-permute-done((bf16[448,768]{1,0:T(8,128)(2,1)}, bf16[448,768]{1,0:T(8,128)(2,1)}, u32[]{:S(2)}, u32[]{:S(2)}) %collective-permute-start.41) | collective-permute-done | bytes 688160 | tf_op jit(solution)/shard_map/ppermute | solution.py:43
  406.4 4.3 maximum_select_fusion.2
  414.8 3.8 collective-permute-done.47
  423.1 5.8 %collective-permute-done.48 = bf16[208,576]{1,0:T(8,128)(2,1)S(1)} collective-permute-done((bf16[208,576]{1,0:T(8,128)(2,1)S(1)}, bf16[208,576]{1,0:T(8,128)(2,1)S(1)}, u32[]{:S(2)}, u32[]{:S(2)}) %collective-permute-start.48) | collective-permute-done | bytes 239648 | tf_op jit(solution)/shard_map/ppermute | solution.py:26
  432.1 14.1 %collective-permute-done.49 = bf16[208,576]{1,0:T(8,128)(2,1)S(1)} collective-permute-done((bf16[208,576]{1,0:T(8,128)(2,1)S(1)}, bf16[208,576]{1,0:T(8,128)(2,1)S(1)}, u32[]{:S(2)}, u32[]{:S(2)}) %collective-permute-start.49) | collective-permute-done | bytes 239648 | tf_op jit(solution)/shard_map/ppermute | solution.py:26
  446.8 8.3 %collective-permute-done.50 = bf16[208,576]{1,0:T(8,128)(2,1)S(1)} collective-permute-done((bf16[208,576]{1,0:T(8,128)(2,1)S(1)}, bf16[208,576]{1,0:T(8,128)(2,1)S(1)}, u32[]{:S(2)}, u32[]{:S(2)}) %collective-permute-start.50) | collective-permute-done | bytes 239648 | tf_op jit(solution)/shard_map/ppermute | solution.py:26
  (322 shorter events, 175.0 us)
Async XLA Ops:
  0.6 62.7 %collective-permute-start.7 = (bf16[512,768]{1,0:T(8,128)(2,1)}, bf16[512,768]{1,0:T(8,128)(2,1)}, u32[]{:S(2)}, u32[]{:S(2)}) collective-permute-start(bf16[512,768]{1,0:T(8,128)(2,1)} %bitcast.263), channel_id=1, source_target_pairs={{0,8},{4,12},{8,0},{12,4},{16,24},{20,28},{24,16},{28,20},{1,9},{5... | collective-permute-start | bytes 2359304 | tf_op jit(solution)/shard_map/ppermute | solution.py:26
  0.7 64.6 %collective-permute-start.8 = (bf16[512,768]{1,0:T(8,128)(2,1)}, bf16[512,768]{1,0:T(8,128)(2,1)}, u32[]{:S(2)}, u32[]{:S(2)}) collective-permute-start(bf16[512,768]{1,0:T(8,128)(2,1)} %bitcast.264), channel_id=1, source_target_pairs={{0,16},{4,20},{8,24},{12,28},{16,0},{20,4},{24,8},{28,12},{1,17},{... | collective-permute-start | bytes 2359304 | tf_op jit(solution)/shard_map/ppermute | solution.py:26
  3.8 68.4 %collective-permute-start.9 = (bf16[512,768]{1,0:T(8,128)(2,1)}, bf16[512,768]{1,0:T(8,128)(2,1)}, u32[]{:S(2)}, u32[]{:S(2)}) collective-permute-start(bf16[512,768]{1,0:T(8,128)(2,1)} %bitcast.265), channel_id=1, source_target_pairs={{0,24},{4,28},{8,16},{12,20},{16,8},{20,12},{24,0},{28,4},{1,25},{... | collective-permute-start | bytes 2359304 | tf_op jit(solution)/shard_map/ppermute | solution.py:26
  20.5 28.9 %collective-permute-start.3 = (bf16[192,3072]{1,0:T(8,128)(2,1)S(1)}, bf16[192,3072]{1,0:T(8,128)(2,1)S(1)}, u32[]{:S(2)}, u32[]{:S(2)}) collective-permute-start(bf16[192,3072]{1,0:T(8,128)(2,1)S(1)} %copy-done.5), channel_id=1, source_target_pairs={{0,2},{1,3},{2,0},{3,1},{4,6},{5,7},{6,4},{7,5},{8,10},{9,11},{10,... | collective-permute-start | bytes 3538952 | tf_op jit(solution)/shard_map/ppermute | solution.py:43
  51.2 36.2 %collective-permute-start.6 = (bf16[2,192,3072]{2,1,0:T(8,128)(2,1)}, bf16[2,192,3072]{2,1,0:T(8,128)(2,1)}, u32[]{:S(2)}, u32[]{:S(2)}) collective-permute-start(bf16[2,192,3072]{2,1,0:T(8,128)(2,1)} %maximum_select_fusion.4), channel_id=1, source_target_pairs={{0,1},{1,0},{2,3},{3,2},{4,5},{5,4},{6,7},{7,6},{8,9},{9,8},{10,11... | collective-permute-start | bytes 7077896 | tf_op jit(solution)/shard_map/ppermute | solution.py:43
  55.4 27.5 %collective-permute-start.16 = (bf16[768,768]{1,0:T(8,128)(2,1)S(1)}, bf16[768,768]{1,0:T(8,128)(2,1)S(1)}, u32[]{:S(2)}, u32[]{:S(2)}) collective-permute-start(bf16[768,768]{1,0:T(8,128)(2,1)S(1)} %copy-done.4), channel_id=1, source_target_pairs={{0,2},{1,3},{2,0},{3,1},{4,6},{5,7},{6,4},{7,5},{8,10},{9,11},{10,... | collective-permute-start | bytes 3538952 | tf_op jit(solution)/shard_map/ppermute | solution.py:43
  65.3 28.0 %collective-permute-start.10 = (bf16[2,3,64,512]{3,2,1,0:T(8,128)(2,1)S(1)}, bf16[2,3,64,512]{3,2,1,0:T(8,128)(2,1)S(1)}, u32[]{:S(2)}, u32[]{:S(2)}) collective-permute-start(bf16[2,3,64,512]{3,2,1,0:T(8,128)(2,1)S(1)} %bitcast.220), channel_id=1, source_target_pairs={{0,4},{4,0},{8,12},{12,8},{16,20},{20,16},{24,28},{28,24},{1,5},{5... | collective-permute-start | bytes 1179656 | tf_op jit(solution)/shard_map/ppermute | solution.py:34
  84.7 57.8 %collective-permute-start.17 = (bf16[2,768,768]{2,1,0:T(8,128)(2,1)}, bf16[2,768,768]{2,1,0:T(8,128)(2,1)}, u32[]{:S(2)}, u32[]{:S(2)}) collective-permute-start(bf16[2,768,768]{2,1,0:T(8,128)(2,1)} %maximum_select_fusion.6), channel_id=1, source_target_pairs={{0,1},{1,0},{2,3},{3,2},{4,5},{5,4},{6,7},{7,6},{8,9},{9,8},{10,11... | collective-permute-start | bytes 7077896 | tf_op jit(solution)/shard_map/ppermute | solution.py:43
  241.8 29.1 %collective-permute-start.21 = (bf16[2,192,1536]{2,1,0:T(8,128)(2,1)}, bf16[2,192,1536]{2,1,0:T(8,128)(2,1)}, u32[]{:S(2)}, u32[]{:S(2)}) collective-permute-start(bf16[2,192,1536]{2,1,0:T(8,128)(2,1)} %constant_dynamic-slice_fusion.10), channel_id=1, source_target_pairs={{0,4},{4,0},{8,12},{12,8},{16,20},{20,16},{24,28},{28,24},{1,5},{5... | collective-permute-start | bytes 3538952 | tf_op jit(solution)/shard_map/ppermute | solution.py:43
  244.6 36.5 %collective-permute-start.20 = (bf16[1,1024,768]{2,1,0:T(8,128)(2,1)}, bf16[1,1024,768]{2,1,0:T(8,128)(2,1)}, u32[]{:S(2)}, u32[]{:S(2)}) collective-permute-start(bf16[1,1024,768]{2,1,0:T(8,128)(2,1)} %constant_dynamic-slice_fusion.11), channel_id=1, source_target_pairs={{0,2},{1,3},{2,0},{3,1},{4,6},{5,7},{6,4},{7,5},{8,10},{9,11},{10,... | collective-permute-start | bytes 4718600 | tf_op jit(solution)/shard_map/ppermute | solution.py:43
  270.9 36.5 %collective-permute-start.29 = (bf16[2,64,2048]{2,1,0:T(8,128)(2,1)}, bf16[2,64,2048]{2,1,0:T(8,128)(2,1)}, u32[]{:S(2)}, u32[]{:S(2)}) collective-permute-start(bf16[2,64,2048]{2,1,0:T(8,128)(2,1)} %bitcast.269), channel_id=1, source_target_pairs={{0,4},{4,0},{8,12},{12,8},{16,20},{20,16},{24,28},{28,24},{1,5},{5... | collective-permute-start | bytes 1572872 | tf_op jit(solution)/shard_map/ppermute | solution.py:34
  307.3 25.5 %collective-permute-start.27 = (bf16[448,768]{1,0:T(8,128)(2,1)}, bf16[448,768]{1,0:T(8,128)(2,1)}, u32[]{:S(2)}, u32[]{:S(2)}) collective-permute-start(bf16[448,768]{1,0:T(8,128)(2,1)} %constant_dynamic-slice_fusion.3), channel_id=1, source_target_pairs={{0,8},{4,12},{8,0},{12,4},{16,24},{20,28},{24,16},{28,20},{1,9},{5... | collective-permute-start | bytes 2064392 | tf_op jit(solution)/shard_map/ppermute | solution.py:43
  307.3 27.8 %collective-permute-start.28 = (bf16[2,64,2048]{2,1,0:T(8,128)(2,1)}, bf16[2,64,2048]{2,1,0:T(8,128)(2,1)}, u32[]{:S(2)}, u32[]{:S(2)}) collective-permute-start(bf16[2,64,2048]{2,1,0:T(8,128)(2,1)} %bitcast.56), channel_id=1, source_target_pairs={{0,4},{4,0},{8,12},{12,8},{16,20},{20,16},{24,28},{28,24},{1,5},{5... | collective-permute-start | bytes 1572872 | tf_op jit(solution)/shard_map/ppermute | solution.py:34
  309.8 27.6 %collective-permute-start.30 = (bf16[3,64,512]{2,1,0:T(8,128)(2,1)}, bf16[3,64,512]{2,1,0:T(8,128)(2,1)}, u32[]{:S(2)}, u32[]{:S(2)}) collective-permute-start(bf16[3,64,512]{2,1,0:T(8,128)(2,1)} %get-tuple-element.228), channel_id=1, source_target_pairs={{0,8},{4,12},{8,0},{12,4},{16,24},{20,28},{24,16},{28,20},{1,9},{5... | collective-permute-start | bytes 589832 | tf_op jit(solution)/shard_map/ppermute | solution.py:26
  311.4 28.8 %collective-permute-start.31 = (bf16[3,64,512]{2,1,0:T(8,128)(2,1)S(1)}, bf16[3,64,512]{2,1,0:T(8,128)(2,1)}, u32[]{:S(2)}, u32[]{:S(2)}) collective-permute-start(bf16[3,64,512]{2,1,0:T(8,128)(2,1)S(1)} %get-tuple-element.229), channel_id=1, source_target_pairs={{0,16},{4,20},{8,24},{12,28},{16,0},{20,4},{24,8},{28,12},{1,17},{... | collective-permute-start | bytes 589832 | tf_op jit(solution)/shard_map/ppermute | solution.py:26
  312.8 28.5 %collective-permute-start.32 = (bf16[3,64,512]{2,1,0:T(8,128)(2,1)S(1)}, bf16[3,64,512]{2,1,0:T(8,128)(2,1)}, u32[]{:S(2)}, u32[]{:S(2)}) collective-permute-start(bf16[3,64,512]{2,1,0:T(8,128)(2,1)S(1)} %get-tuple-element.226), channel_id=1, source_target_pairs={{0,24},{4,28},{8,16},{12,20},{16,8},{20,12},{24,0},{28,4},{1,25},{... | collective-permute-start | bytes 589832 | tf_op jit(solution)/shard_map/ppermute | solution.py:26
  332.8 36.9 %collective-permute-start.35 = (bf16[192,2304]{1,0:T(8,128)(2,1)S(1)}, bf16[192,2304]{1,0:T(8,128)(2,1)S(1)}, u32[]{:S(2)}, u32[]{:S(2)}) collective-permute-start(bf16[192,2304]{1,0:T(8,128)(2,1)S(1)} %copy-done.3), channel_id=1, source_target_pairs={{0,2},{1,3},{2,0},{3,1},{4,6},{5,7},{6,4},{7,5},{8,10},{9,11},{10,... | collective-permute-start | bytes 2654216 | tf_op jit(solution)/shard_map/ppermute | solution.py:43
  341.3 28.4 %collective-permute-start.38 = (bf16[3,64,512]{2,1,0:T(8,128)(2,1)}, bf16[3,64,512]{2,1,0:T(8,128)(2,1)S(1)}, u32[]{:S(2)}, u32[]{:S(2)}) collective-permute-start(bf16[3,64,512]{2,1,0:T(8,128)(2,1)} %get-tuple-element.222), channel_id=1, source_target_pairs={{0,24},{4,28},{8,16},{12,20},{16,8},{20,12},{24,0},{28,4},{1,25},{... | collective-permute-start | bytes 589832 | tf_op jit(solution)/shard_map/ppermute | solution.py:26
  344.3 37.2 %collective-permute-start.33 = (bf16[448,768]{1,0:T(8,128)(2,1)}, bf16[448,768]{1,0:T(8,128)(2,1)}, u32[]{:S(2)}, u32[]{:S(2)}) collective-permute-start(bf16[448,768]{1,0:T(8,128)(2,1)} %add_convert_fusion.6), channel_id=1, source_target_pairs={{0,16},{4,20},{8,24},{12,28},{16,0},{20,4},{24,8},{28,12},{1,17},{... | collective-permute-start | bytes 2064392 | tf_op jit(solution)/shard_map/ppermute | solution.py:43
  412.4 48.3 %collective-permute-start.44 = (bf16[3,64,512]{2,1,0:T(8,128)(2,1)}, bf16[3,64,512]{2,1,0:T(8,128)(2,1)}, u32[]{:S(2)}, u32[]{:S(2)}) collective-permute-start(bf16[3,64,512]{2,1,0:T(8,128)(2,1)} %get-tuple-element.218), channel_id=1, source_target_pairs={{0,8},{4,12},{8,0},{12,4},{16,24},{20,28},{24,16},{28,20},{1,9},{5... | collective-permute-start | bytes 589832 | tf_op jit(solution)/shard_map/ppermute | solution.py:26
  414.1 47.0 %collective-permute-start.43 = (bf16[896,768]{1,0:T(8,128)(2,1)S(1)}, bf16[896,768]{1,0:T(8,128)(2,1)}, u32[]{:S(2)}, u32[]{:S(2)}) collective-permute-start(bf16[896,768]{1,0:T(8,128)(2,1)S(1)} %maximum_select_fusion.10), channel_id=1, source_target_pairs={{0,4},{4,0},{8,12},{12,8},{16,20},{20,16},{24,28},{28,24},{1,5},{5... | collective-permute-start | bytes 4128776 | tf_op jit(solution)/shard_map/ppermute | solution.py:43
  420.3 25.9 %collective-permute-start.49 = (bf16[208,576]{1,0:T(8,128)(2,1)S(1)}, bf16[208,576]{1,0:T(8,128)(2,1)S(1)}, u32[]{:S(2)}, u32[]{:S(2)}) collective-permute-start(bf16[208,576]{1,0:T(8,128)(2,1)S(1)} %fusion.8), channel_id=1, source_target_pairs={{0,16},{4,20},{8,24},{12,28},{16,0},{20,4},{24,8},{28,12},{1,17},{... | collective-permute-start | bytes 718856 | tf_op jit(solution)/shard_map/ppermute | solution.py:26
  421.8 33.3 %collective-permute-start.50 = (bf16[208,576]{1,0:T(8,128)(2,1)S(1)}, bf16[208,576]{1,0:T(8,128)(2,1)S(1)}, u32[]{:S(2)}, u32[]{:S(2)}) collective-permute-start(bf16[208,576]{1,0:T(8,128)(2,1)S(1)} %fusion.8), channel_id=1, source_target_pairs={{0,24},{4,28},{8,16},{12,20},{16,8},{20,12},{24,0},{28,4},{1,25},{... | collective-permute-start | bytes 718856 | tf_op jit(solution)/shard_map/ppermute | solution.py:26
  428.9 31.8 %collective-permute-start.45 = (bf16[3,64,512]{2,1,0:T(8,128)(2,1)}, bf16[3,64,512]{2,1,0:T(8,128)(2,1)}, u32[]{:S(2)}, u32[]{:S(2)}) collective-permute-start(bf16[3,64,512]{2,1,0:T(8,128)(2,1)} %get-tuple-element.217), channel_id=1, source_target_pairs={{0,16},{4,20},{8,24},{12,28},{16,0},{20,4},{24,8},{28,12},{1,17},{... | collective-permute-start | bytes 589832 | tf_op jit(solution)/shard_map/ppermute | solution.py:26
  (78 other events, 639.3 us)

commit v3 on v1

--- a/solution.py
+++ b/solution.py
@@ -245,11 +245,11 @@
 
     lax.fori_loop(0, groups, one_slot, 0)
     g, s = meta[0], meta[1]
-    for j in range(groups):
+
+    def finish(j, carry):
+        at = pl.ds(pl.multiple_of(j * rows, rows), rows)
         for e in range(parts):
-            block = (g ^ j) * parts + lax.rem(s - e + parts, parts)
-            terms = accum_ref[block].T
-            at = slice(j * rows, (j + 1) * rows)
+            terms = accum_ref[(g ^ j) * parts + lax.rem(s - e + parts, parts)].T
             d_key = terms[:HD] * HD**-0.5
             d_value = terms[HD:]
             if e == 0:
@@ -258,6 +258,9 @@
             else:
                 theirs[e - 1, 0, :, at] = d_key.astype(jnp.bfloat16)
                 theirs[e - 1, 1, :, at] = d_value.astype(jnp.bfloat16)
+        return carry
+
+    lax.fori_loop(0, groups, finish, 0)
 
 
 def head_block(head, *shape):
@@ -378,7 +381,7 @@
 
 def over_blocks(count, aligned, step, value):
     if aligned:
-        return lax.fori_loop(0, count, step, value)
+        return lax.fori_loop(0, count, step, value, unroll=4)
     for i in range(count):
         value = step(i, value)
     return value
@@ -559,11 +562,18 @@
     slots, (d_qkv, send, keep, total) = refs[:-4], refs[-4:]
     rows = slots[0].shape[0]
     shard = send.shape[1] - PAD
-    value = None
-    for j, slot in enumerate(slots):
-        term = dot_t(slot[...].T, d_qkv[:, j * rows : (j + 1) * rows])
-        value = term if value is None else value + term
-    total[...] = value
+    size = math.gcd(total.shape[0], 256)
+
+    def step(i, carry):
+        at = pl.ds(pl.multiple_of(i * size, size), size)
+        value = None
+        for j, slot in enumerate(slots):
+            term = dot_t(slot[:, at].T, d_qkv[:, j * rows : (j + 1) * rows])
+            value = term if value is None else value + term
+        total[at] = value
+        return carry
+
+    lax.fori_loop(0, total.shape[0] // size, step, 0)
     ones = jnp.ones((PAD, d_qkv.shape[1]), jnp.bfloat16)
     sums = dot_t(ones, d_qkv[...]).astype(jnp.bfloat16)
     for side, ref in enumerate((send, keep)):
@@ -632,7 +642,9 @@
 
     slots = gather_groups(tokens, groups, parts)
 
-    own_cols = pick(qkv_weight.reshape(shard, 3, groups, span), g, 2).reshape(shard, width)
+    own_cols = jnp.concatenate(
+        [lax.dynamic_slice_in_dim(qkv_weight, i * model + g * span, span, 1) for i in range(3)], axis=1
+    )
     small = jnp.concatenate(
         [
             query_bias, value_bias, out_bias, norm1_gain, norm1_bias,
@@ -817,12 +829,18 @@
     qkv_low = qkv_sum[0]
     by_group = jnp.zeros((groups,) + qkv_low.shape, bf16)
     turns = [ctx_swap(qkv_low, groups, parts, j) if j else qkv_low for j in range(groups)]
-    other, *late = together(other, *late)
-    turns = together(*turns)
+    lower_rows = (inner_shard + shard + line_rows) // 2
+    lower = join(bit_at("ctx", 0), merged[:lower_rows], other[:lower_rows], 0)
+    wide_half = lambda m: jnp.concatenate(
+        [m[lower_rows + c * shard : lower_rows + (c + 1) * shard] for c in range(chunks)], axis=1
+    )
+    upper = join(bit_at("ctx", 0), wide_half(merged), wide_half(other), 1)
+    lower, upper, *turns = together(lower.astype(f32), upper.astype(f32), *turns)
     for j, piece in enumerate(turns):
         by_group = lax.dynamic_update_slice(by_group, piece[None], (g ^ j, 0, 0))
-    natural = by_group.reshape(groups, shard + PAD, 3, span).transpose(1, 2, 0, 3)
-    natural = natural.reshape(shard + PAD, 3 * model).astype(f32)
+    natural = jnp.concatenate(
+        [by_group[b, :, i * span : (i + 1) * span] for i in range(3) for b in range(groups)], axis=1
+    ).astype(f32)
     grad_qkv_shard = natural[:shard]
     bias_line = natural[shard]
     grad_query_shift = lax.dynamic_slice(bias_line, (f * shard,), (shard,))
@@ -838,13 +856,6 @@
         (((0,), (1,)), ((), ())),
         preferred_element_type=f32,
     )
-
-    lower_rows = (inner_shard + shard + line_rows) // 2
-    lower = join(bit_at("ctx", 0), merged[:lower_rows], other[:lower_rows], 0)
-    wide_half = lambda m: jnp.concatenate(
-        [m[lower_rows + c * shard : lower_rows + (c + 1) * shard] for c in range(chunks)], axis=1
-    )
-    upper = join(bit_at("ctx", 0), wide_half(merged), wide_half(other), 1)
 
     ends = inner_shard + shard
     flat = lower[ends:].reshape(-1).astype(f32)

time: 467 us -> 447 us (0.957)
  Pallas kernels: 121 us -> 158 us
  starting transfers between devices: 88.5 us -> 55.3 us
  other arithmetic: 63.9 us -> 52 us
  local copies, waits for them, and re-layouts: 55.8 us -> 45.8 us
    ppermute x22, starting transfers between devices: 44.4 us -> 19.2 us  [swap(): return lax.ppermute(array, axis, [(i, i ^ 1 << bit) for i in range(size)])]
    pallas_call x3, Pallas kernels: 39.8 us -> 62.7 us  [attend_back(): pl.pallas_call(partial(attend_back_kernel, groups, parts, docs, rows), gr...]
    pallas_call x1, Pallas kernels: 26.5 us -> 46.3 us  [attend(): pl.pallas_call(partial(attend_kernel, groups, parts, docs, rows), grid_sp...]
    select_n x17 -> x16, other arithmetic: 29.8 us -> 21.6 us  [join(): jnp.where(mine == 0, jnp.concatenate([own, other], axis=dim), jnp.concate...]
    ppermute x8, starting transfers between devices: 15.9 us -> 8.95 us  [part_shift(): return lax.ppermute(array, 'ctx', pairs)]
    pallas_call x1, Pallas kernels: 34.6 us -> 28 us  [feed_forward(): pl.pallas_call(feed_kernel, grid=(rows // tile,), in_specs=[by_rows(model...]
    concatenate x1, local copies, waits for them, and re-layouts: 0.09 us -> 6.1 us  [body(): jnp.concatenate([query_bias, value_bias, out_bias, norm1_gain, norm1_bias...]
    unnamed x130 -> x89, local copies, waits for them, and re-layouts: 10.1 us -> 7.98 us
  transfers between devices with their start and end apart: 51 -> 51, of which waited for: 22 -> 23; matrix products, arithmetic and copies ran while one was open for 21% -> 20% of each run, Pallas kernels for 16% -> 27%
where the time goes in v3:
time: 447 us; the launch traced here: 441 us
  Pallas kernels  158 us (35%)
  waiting for transfers between devices  117 us (26%)
  starting transfers between devices  55.3 us (12%)
  other arithmetic  52 us (12%)
  local copies, waits for them, and re-layouts  45.8 us (10%)
  matrix products  11 us (2%)
    pallas_call x3, Pallas kernels, attend_back(): pl.pallas_call(partial(attend_back_kernel, groups, parts, docs, rows), gr...  62.7 us
    ppermute x22, waiting for transfers between devices, swap(): return lax.ppermute(array, axis, [(i, i ^ 1 << bit) for i in range(size)])  53.9 us
    ppermute x21, waiting for transfers between devices, ctx_swap(): return lax.ppermute(array, 'ctx', pairs)  53 us
    pallas_call x1, Pallas kernels, attend(): pl.pallas_call(partial(attend_kernel, groups, parts, docs, rows), grid_sp...  46.3 us
    pallas_call x1, Pallas kernels, feed_forward(): pl.pallas_call(feed_kernel, grid=(rows // tile,), in_specs=[by_rows(model...  28 us
    ppermute x21, starting transfers between devices, ctx_swap(): return lax.ppermute(array, 'ctx', pairs)  27.2 us
    select_n x16, other arithmetic, join(): jnp.where(mine == 0, jnp.concatenate([own, other], axis=dim), jnp.concate...  21.6 us
    ppermute x22, starting transfers between devices, swap(): return lax.ppermute(array, axis, [(i, i ^ 1 << bit) for i in range(size)])  19.2 us
  transfers between devices with their start and end apart: 51, of which 23 were waited for; matrix products, arithmetic and copies ran while one was open for 20% of the time, Pallas kernels for 27%

profile of v3, /device:TPU:8, one launch (start us, length us, event | category | flops | bytes accessed | tf_op | source)
XLA Modules:
  0.0 441.2 jit_solution(14711251776525247147)
XLA Ops:
  4.2 6.1 %concatenate.232 = bf16[2304]{0:T(1024)(128)(2,1)S(1)} concatenate(bf16[192]{0:T(256)(128)(2,1)} %param.19, bf16[192]{0:T(256)(128)(2,1)} %param.20, bf16[192]{0:T(256)(128)(2,1)} %param.22, bf16[192]{0:T(256)(128)(2,1)} %param.23, bf16[192]{0:T(256)(128)(2,1)} %param.24, bf16[192]{0:T(256)(128)(2,1)} %param.28, bf16[192]{0:T(256)(128)(2,1)} %param.29, bf16[192]{0:T(256)(128)(2,1)} %param.30, ...), dimensions={0} | concatenate | bytes 9216 | tf_op jit(solution)/shard_map/concatenate | solution.py:648
  15.1 4.1 collective-permute-done
  32.8 8.9 %collective-permute-done.5.refs_4_ = bf16[2,3,64,512]{3,2,1,0:T(8,128)(2,1)S(1)} collective-permute-done((bf16[2,3,64,512]{3,2,1,0:T(8,128)(2,1)S(1)}, bf16[2,3,64,512]{3,2,1,0:T(8,128)(2,1)S(1)}, u32[]{:S(2)}, u32[]{:S(2)}) %collective-permute-start.5) | collective-permute-done | bytes 393248 | tf_op jit(solution)/shard_map/ppermute | solution.py:34
  43.2 6.1 %collective-permute-done.3 = bf16[192,3072]{1,0:T(8,128)(2,1)S(1)} collective-permute-done((bf16[192,3072]{1,0:T(8,128)(2,1)S(1)}, bf16[192,3072]{1,0:T(8,128)(2,1)S(1)}, u32[]{:S(2)}, u32[]{:S(2)}) %collective-permute-start.3) | collective-permute-done | bytes 1179680 | tf_op jit(solution)/shard_map/ppermute | solution.py:43
  51.7 3.6 collective-permute-done.1
  68.7 3.4 collective-permute-done.9.refs_3_
  77.5 5.3 %collective-permute-done.16 = bf16[768,768]{1,0:T(8,128)(2,1)S(1)} collective-permute-done((bf16[768,768]{1,0:T(8,128)(2,1)S(1)}, bf16[768,768]{1,0:T(8,128)(2,1)S(1)}, u32[]{:S(2)}, u32[]{:S(2)}) %collective-permute-start.16) | collective-permute-done | bytes 1179680 | tf_op jit(solution)/shard_map/ppermute | solution.py:43
  94.5 46.3 %attend.1 = (bf16[3,64,2048]{2,1,0:T(8,128)(2,1)}, f32[3,64,2048]{2,1,0:T(8,128)}, f32[3,1,2048]{2,1,0:T(1,128)}) custom-call(s32[18]{0:T(128)} %pad_add_fusion.2.meta, bf16[3,3,64,512]{3,2,1,0:T(8,128)(2,1)} %bitcast.226, bf16[3,3,64,512]{3,2,1,0:T(8,128)(2,1)} %bitcast.230, bf16[3,3,64,512]{3,2,1,0:T(8,128)(2,1)} %bitcast.234, ...), custom_call_target="tpu_custom_call" | custom-call | flops 17999998976 | bytes 60000000 | tf_op jit(solution)/shard_map/attend/pallas_call | solution.py:293
  159.2 28.0 %feed_forward.1 = (bf16[512,768]{1,0:T(8,128)(2,1)}, f32[512,768]{1,0:T(8,128)}, bf16[768,512]{1,0:T(8,128)(2,1)}, bf16[4,512,192]{2,1,0:T(8,128)(2,1)}, bf16[4,...) custom-call(bf16[512,768]{1,0:T(8,128)(2,1)} %bitcast.268, ...), custom_call_target="tpu_custom_call" | custom-call | flops 10871635968 | bytes 30000000 | tf_op jit(solution)/shard_map/feed_forward/pallas_call | solution.py:488
  191.2 12.5 %weight_grads.1 = (bf16[2,1024,768]{2,1,0:T(8,128)(2,1)}, bf16[2,192,3072]{2,1,0:T(8,128)(2,1)}, bf16[2,1024,768]{2,1,0:T(8,128)(2,1)}, bf16[2,192,3072]{2,1,0:T(8,128)(2,1)}) custom-call(s32[2]{0:T(128)} %pad_add_fusion.3.which, bf16[4,512,768]{2,1,0:T(8,128)(2,1)} %get-tuple-element.118.refs_0_.refs_4_, ...), custom_call_target="tpu_custom_call" | custom-call | flops 5435817984 | bytes 25000000 | tf_op jit(solution)/shard_map/weight_grads/pallas_call | solution.py:545
  218.3 3.5 collective-permute-done.23.refs_10_
  221.7 4.0 collective-permute-done.24.refs_11_
  226.4 20.9 %attend_back.5 = (bf16[64,2048]{1,0:T(8,128)(2,1)}, f32[2,64,2048]{2,1,0:T(8,128)}, bf16[1,2,64,2048]{3,2,1,0:T(8,128)(2,1)}) custom-call(s32[18]{0:T(128)} %pad_add_fusion.2.meta, bf16[3,3,64,512]{3,2,1,0:T(8,128)(2,1)} %bitcast.227, bf16[3,3,64,512]{3,2,1,0:T(8,128)(2,1)} %bitcast.231, bf16[3,3,64,512]{3,2,1,0:T(8,128)(2,1)} %bitcast.235, ...), custom_call_target="tpu_custom_call" | custom-call | flops 15000000512 | bytes 20000000 | tf_op jit(solution)/shard_map/attend_back/pallas_call | solution.py:340
  249.3 5.8 %collective-permute-done.20 = bf16[1,1024,768]{2,1,0:T(8,128)(2,1)} collective-permute-done((bf16[1,1024,768]{2,1,0:T(8,128)(2,1)}, bf16[1,1024,768]{2,1,0:T(8,128)(2,1)}, u32[]{:S(2)}, u32[]{:S(2)}) %collective-permute-start.20) | collective-permute-done | bytes 1572896 | tf_op jit(solution)/shard_map/ppermute | solution.py:43
  260.2 20.9 %attend_back.3 = (bf16[64,2048]{1,0:T(8,128)(2,1)}, f32[2,64,2048]{2,1,0:T(8,128)}, bf16[1,2,64,2048]{3,2,1,0:T(8,128)(2,1)}) custom-call(s32[18]{0:T(128)} %pad_add_fusion.2.meta, bf16[3,3,64,512]{3,2,1,0:T(8,128)(2,1)} %bitcast.228, bf16[3,3,64,512]{3,2,1,0:T(8,128)(2,1)} %bitcast.232, bf16[3,3,64,512]{3,2,1,0:T(8,128)(2,1)} %bitcast.236, ...), custom_call_target="tpu_custom_call" | custom-call | flops 15000000512 | bytes 20000000 | tf_op jit(solution)/shard_map/attend_back/pallas_call | solution.py:340
  290.0 20.9 %attend_back.4 = (bf16[64,2048]{1,0:T(8,128)(2,1)}, f32[2,64,2048]{2,1,0:T(8,128)}, bf16[1,2,64,2048]{3,2,1,0:T(8,128)(2,1)}) custom-call(s32[18]{0:T(128)} %pad_add_fusion.2.meta, bf16[3,3,64,512]{3,2,1,0:T(8,128)(2,1)} %bitcast.229, bf16[3,3,64,512]{3,2,1,0:T(8,128)(2,1)} %bitcast.233, bf16[3,3,64,512]{3,2,1,0:T(8,128)(2,1)} %bitcast.237, ...), custom_call_target="tpu_custom_call" | custom-call | flops 15000000512 | bytes 20000000 | tf_op jit(solution)/shard_map/attend_back/pallas_call | solution.py:340
  322.5 3.7 collective-permute-start.33
  328.3 8.1 %qkv_grads.1 = (bf16[2,208,576]{2,1,0:T(8,128)(2,1)}, bf16[2,208,576]{2,1,0:T(8,128)(2,1)}) custom-call(s32[2]{0:T(128)} %pad_add_fusion.3.which, bf16[512,768]{1,0:T(8,128)(2,1)} %bitcast.269, bf16[512,768]{1,0:T(8,128)(2,1)} %collective-permute-done.7.refs_1_, bf16[512,768]{1,0:T(8,128)(2,1)} %collective-permute-done.8.refs_2_, ...), custom_call_target="tpu_custom_call" | custom-call | flops 1811939328 | bytes 8000000 | tf_op jit(solution)/shard_map/qkv_grads/pallas_call | solution.py:591
  336.5 5.5 %collective-permute-done.37 = bf16[3,64,512]{2,1,0:T(8,128)(2,1)} collective-permute-done((bf16[3,64,512]{2,1,0:T(8,128)(2,1)}, bf16[3,64,512]{2,1,0:T(8,128)(2,1)}, u32[]{:S(2)}, u32[]{:S(2)}) %collective-permute-start.37) | collective-permute-done | bytes 196640 | tf_op jit(solution)/shard_map/ppermute | solution.py:26
  341.9 5.3 %collective-permute-done.38 = bf16[3,64,512]{2,1,0:T(8,128)(2,1)} collective-permute-done((bf16[3,64,512]{2,1,0:T(8,128)(2,1)}, bf16[3,64,512]{2,1,0:T(8,128)(2,1)}, u32[]{:S(2)}, u32[]{:S(2)}) %collective-permute-start.38) | collective-permute-done | bytes 196640 | tf_op jit(solution)/shard_map/ppermute | solution.py:26
  347.3 11.7 %collective-permute-done.33 = bf16[448,768]{1,0:T(8,128)(2,1)} collective-permute-done((bf16[448,768]{1,0:T(8,128)(2,1)}, bf16[448,768]{1,0:T(8,128)(2,1)}, u32[]{:S(2)}, u32[]{:S(2)}) %collective-permute-start.33) | collective-permute-done | bytes 688160 | tf_op jit(solution)/shard_map/ppermute | solution.py:43
  369.4 17.8 %collective-permute-done.39 = bf16[3,64,512]{2,1,0:T(8,128)(2,1)S(1)} collective-permute-done((bf16[3,64,512]{2,1,0:T(8,128)(2,1)S(1)}, bf16[3,64,512]{2,1,0:T(8,128)(2,1)S(1)}, u32[]{:S(2)}, u32[]{:S(2)}) %collective-permute-start.39) | collective-permute-done | bytes 196640 | tf_op jit(solution)/shard_map/ppermute | solution.py:26
  408.7 13.8 %collective-permute-done.46 = bf16[896,768]{1,0:T(8,128)(2,1)S(1)} collective-permute-done((bf16[896,768]{1,0:T(8,128)(2,1)S(1)}, bf16[896,768]{1,0:T(8,128)(2,1)S(1)}, u32[]{:S(2)}, u32[]{:S(2)}) %collective-permute-start.46) | collective-permute-done | bytes 1376288 | tf_op jit(solution)/shard_map/ppermute | solution.py:43
  424.8 4.0 collective-permute-done.50
  (306 shorter events, 169.0 us)
Async XLA Ops:
  0.7 62.5 %collective-permute-start.7 = (bf16[512,768]{1,0:T(8,128)(2,1)}, bf16[512,768]{1,0:T(8,128)(2,1)}, u32[]{:S(2)}, u32[]{:S(2)}) collective-permute-start(bf16[512,768]{1,0:T(8,128)(2,1)} %bitcast.265), channel_id=1, source_target_pairs={{0,8},{4,12},{8,0},{12,4},{16,24},{20,28},{24,16},{28,20},{1,9},{5... | collective-permute-start | bytes 2359304 | tf_op jit(solution)/shard_map/ppermute | solution.py:26
  0.7 64.4 %collective-permute-start.8 = (bf16[512,768]{1,0:T(8,128)(2,1)}, bf16[512,768]{1,0:T(8,128)(2,1)}, u32[]{:S(2)}, u32[]{:S(2)}) collective-permute-start(bf16[512,768]{1,0:T(8,128)(2,1)} %bitcast.266), channel_id=1, source_target_pairs={{0,16},{4,20},{8,24},{12,28},{16,0},{20,4},{24,8},{28,12},{1,17},{... | collective-permute-start | bytes 2359304 | tf_op jit(solution)/shard_map/ppermute | solution.py:26
  3.8 68.4 %collective-permute-start.9 = (bf16[512,768]{1,0:T(8,128)(2,1)}, bf16[512,768]{1,0:T(8,128)(2,1)}, u32[]{:S(2)}, u32[]{:S(2)}) collective-permute-start(bf16[512,768]{1,0:T(8,128)(2,1)} %bitcast.267), channel_id=1, source_target_pairs={{0,24},{4,28},{8,16},{12,20},{16,8},{20,12},{24,0},{28,4},{1,25},{... | collective-permute-start | bytes 2359304 | tf_op jit(solution)/shard_map/ppermute | solution.py:26
  20.4 28.9 %collective-permute-start.3 = (bf16[192,3072]{1,0:T(8,128)(2,1)S(1)}, bf16[192,3072]{1,0:T(8,128)(2,1)S(1)}, u32[]{:S(2)}, u32[]{:S(2)}) collective-permute-start(bf16[192,3072]{1,0:T(8,128)(2,1)S(1)} %copy-done.5), channel_id=1, source_target_pairs={{0,2},{1,3},{2,0},{3,1},{4,6},{5,7},{6,4},{7,5},{8,10},{9,11},{10,... | collective-permute-start | bytes 3538952 | tf_op jit(solution)/shard_map/ppermute | solution.py:43
  51.1 36.2 %collective-permute-start.6 = (bf16[2,192,3072]{2,1,0:T(8,128)(2,1)}, bf16[2,192,3072]{2,1,0:T(8,128)(2,1)}, u32[]{:S(2)}, u32[]{:S(2)}) collective-permute-start(bf16[2,192,3072]{2,1,0:T(8,128)(2,1)} %maximum_select_fusion.4), channel_id=1, source_target_pairs={{0,1},{1,0},{2,3},{3,2},{4,5},{5,4},{6,7},{7,6},{8,9},{9,8},{10,11... | collective-permute-start | bytes 7077896 | tf_op jit(solution)/shard_map/ppermute | solution.py:43
  55.3 27.5 %collective-permute-start.16 = (bf16[768,768]{1,0:T(8,128)(2,1)S(1)}, bf16[768,768]{1,0:T(8,128)(2,1)S(1)}, u32[]{:S(2)}, u32[]{:S(2)}) collective-permute-start(bf16[768,768]{1,0:T(8,128)(2,1)S(1)} %copy-done.4), channel_id=1, source_target_pairs={{0,2},{1,3},{2,0},{3,1},{4,6},{5,7},{6,4},{7,5},{8,10},{9,11},{10,... | collective-permute-start | bytes 3538952 | tf_op jit(solution)/shard_map/ppermute | solution.py:43
  65.2 27.8 %collective-permute-start.10 = (bf16[2,3,64,512]{3,2,1,0:T(8,128)(2,1)S(1)}, bf16[2,3,64,512]{3,2,1,0:T(8,128)(2,1)S(1)}, u32[]{:S(2)}, u32[]{:S(2)}) collective-permute-start(bf16[2,3,64,512]{3,2,1,0:T(8,128)(2,1)S(1)} %bitcast.221), channel_id=1, source_target_pairs={{0,4},{4,0},{8,12},{12,8},{16,20},{20,16},{24,28},{28,24},{1,5},{5... | collective-permute-start | bytes 1179656 | tf_op jit(solution)/shard_map/ppermute | solution.py:34
  84.6 61.5 %collective-permute-start.17 = (bf16[2,768,768]{2,1,0:T(8,128)(2,1)}, bf16[2,768,768]{2,1,0:T(8,128)(2,1)}, u32[]{:S(2)}, u32[]{:S(2)}) collective-permute-start(bf16[2,768,768]{2,1,0:T(8,128)(2,1)} %maximum_select_fusion.6), channel_id=1, source_target_pairs={{0,1},{1,0},{2,3},{3,2},{4,5},{5,4},{6,7},{7,6},{8,9},{9,8},{10,11... | collective-permute-start | bytes 7077896 | tf_op jit(solution)/shard_map/ppermute | solution.py:43
  217.0 30.3 %collective-permute-start.21 = (bf16[2,192,1536]{2,1,0:T(8,128)(2,1)}, bf16[2,192,1536]{2,1,0:T(8,128)(2,1)}, u32[]{:S(2)}, u32[]{:S(2)}) collective-permute-start(bf16[2,192,1536]{2,1,0:T(8,128)(2,1)} %constant_dynamic-slice_fusion.10), channel_id=1, source_target_pairs={{0,4},{4,0},{8,12},{12,8},{16,20},{20,16},{24,28},{28,24},{1,5},{5... | collective-permute-start | bytes 3538952 | tf_op jit(solution)/shard_map/ppermute | solution.py:43
  218.3 36.8 %collective-permute-start.20 = (bf16[1,1024,768]{2,1,0:T(8,128)(2,1)}, bf16[1,1024,768]{2,1,0:T(8,128)(2,1)}, u32[]{:S(2)}, u32[]{:S(2)}) collective-permute-start(bf16[1,1024,768]{2,1,0:T(8,128)(2,1)} %constant_dynamic-slice_fusion.11), channel_id=1, source_target_pairs={{0,2},{1,3},{2,0},{3,1},{4,6},{5,7},{6,4},{7,5},{8,10},{9,11},{10,... | collective-permute-start | bytes 4718600 | tf_op jit(solution)/shard_map/ppermute | solution.py:43
  247.3 36.9 %collective-permute-start.29 = (bf16[2,64,2048]{2,1,0:T(8,128)(2,1)}, bf16[2,64,2048]{2,1,0:T(8,128)(2,1)}, u32[]{:S(2)}, u32[]{:S(2)}) collective-permute-start(bf16[2,64,2048]{2,1,0:T(8,128)(2,1)} %bitcast.271), channel_id=1, source_target_pairs={{0,4},{4,0},{8,12},{12,8},{16,20},{20,16},{24,28},{28,24},{1,5},{5... | collective-permute-start | bytes 1572872 | tf_op jit(solution)/shard_map/ppermute | solution.py:34
  258.0 24.5 %collective-permute-start.25 = (bf16[1,512,768]{2,1,0:T(8,128)(2,1)S(1)}, bf16[1,512,768]{2,1,0:T(8,128)(2,1)S(1)}, u32[]{:S(2)}, u32[]{:S(2)}) collective-permute-start(bf16[1,512,768]{2,1,0:T(8,128)(2,1)S(1)} %constant_dynamic-slice_fusion.5), channel_id=1, source_target_pairs={{0,4},{4,0},{8,12},{12,8},{16,20},{20,16},{24,28},{28,24},{1,5},{5... | collective-permute-start | bytes 2359304 | tf_op jit(solution)/shard_map/ppermute | solution.py:43
  284.0 27.0 %collective-permute-start.27 = (bf16[448,768]{1,0:T(8,128)(2,1)}, bf16[448,768]{1,0:T(8,128)(2,1)}, u32[]{:S(2)}, u32[]{:S(2)}) collective-permute-start(bf16[448,768]{1,0:T(8,128)(2,1)} %constant_dynamic-slice_fusion.3), channel_id=1, source_target_pairs={{0,8},{4,12},{8,0},{12,4},{16,24},{20,28},{24,16},{28,20},{1,9},{5... | collective-permute-start | bytes 2064392 | tf_op jit(solution)/shard_map/ppermute | solution.py:43
  284.0 29.3 %collective-permute-start.28 = (bf16[2,64,2048]{2,1,0:T(8,128)(2,1)}, bf16[2,64,2048]{2,1,0:T(8,128)(2,1)}, u32[]{:S(2)}, u32[]{:S(2)}) collective-permute-start(bf16[2,64,2048]{2,1,0:T(8,128)(2,1)} %bitcast.56), channel_id=1, source_target_pairs={{0,4},{4,0},{8,12},{12,8},{16,20},{20,16},{24,28},{28,24},{1,5},{5... | collective-permute-start | bytes 1572872 | tf_op jit(solution)/shard_map/ppermute | solution.py:34
  286.5 30.6 %collective-permute-start.30 = (bf16[3,64,512]{2,1,0:T(8,128)(2,1)}, bf16[3,64,512]{2,1,0:T(8,128)(2,1)}, u32[]{:S(2)}, u32[]{:S(2)}) collective-permute-start(bf16[3,64,512]{2,1,0:T(8,128)(2,1)} %get-tuple-element.222), channel_id=1, source_target_pairs={{0,8},{4,12},{8,0},{12,4},{16,24},{20,28},{24,16},{28,20},{1,9},{5... | collective-permute-start | bytes 589832 | tf_op jit(solution)/shard_map/ppermute | solution.py:26
  288.3 31.6 %collective-permute-start.31 = (bf16[3,64,512]{2,1,0:T(8,128)(2,1)}, bf16[3,64,512]{2,1,0:T(8,128)(2,1)}, u32[]{:S(2)}, u32[]{:S(2)}) collective-permute-start(bf16[3,64,512]{2,1,0:T(8,128)(2,1)} %get-tuple-element.223), channel_id=1, source_target_pairs={{0,16},{4,20},{8,24},{12,28},{16,0},{20,4},{24,8},{28,12},{1,17},{... | collective-permute-start | bytes 589832 | tf_op jit(solution)/shard_map/ppermute | solution.py:26
  289.4 31.5 %collective-permute-start.32 = (bf16[3,64,512]{2,1,0:T(8,128)(2,1)}, bf16[3,64,512]{2,1,0:T(8,128)(2,1)}, u32[]{:S(2)}, u32[]{:S(2)}) collective-permute-start(bf16[3,64,512]{2,1,0:T(8,128)(2,1)} %get-tuple-element.220), channel_id=1, source_target_pairs={{0,24},{4,28},{8,16},{12,20},{16,8},{20,12},{24,0},{28,4},{1,25},{... | collective-permute-start | bytes 589832 | tf_op jit(solution)/shard_map/ppermute | solution.py:26
  311.0 36.3 %collective-permute-start.35 = (bf16[192,2304]{1,0:T(8,128)(2,1)S(1)}, bf16[192,2304]{1,0:T(8,128)(2,1)S(1)}, u32[]{:S(2)}, u32[]{:S(2)}) collective-permute-start(bf16[192,2304]{1,0:T(8,128)(2,1)S(1)} %copy-done.3), channel_id=1, source_target_pairs={{0,2},{1,3},{2,0},{3,1},{4,6},{5,7},{6,4},{7,5},{8,10},{9,11},{10,... | collective-permute-start | bytes 2654216 | tf_op jit(solution)/shard_map/ppermute | solution.py:43
  320.9 26.3 %collective-permute-start.38 = (bf16[3,64,512]{2,1,0:T(8,128)(2,1)}, bf16[3,64,512]{2,1,0:T(8,128)(2,1)}, u32[]{:S(2)}, u32[]{:S(2)}) collective-permute-start(bf16[3,64,512]{2,1,0:T(8,128)(2,1)} %get-tuple-element.214), channel_id=1, source_target_pairs={{0,24},{4,28},{8,16},{12,20},{16,8},{20,12},{24,0},{28,4},{1,25},{... | collective-permute-start | bytes 589832 | tf_op jit(solution)/shard_map/ppermute | solution.py:26
  322.5 36.4 %collective-permute-start.33 = (bf16[448,768]{1,0:T(8,128)(2,1)}, bf16[448,768]{1,0:T(8,128)(2,1)}, u32[]{:S(2)}, u32[]{:S(2)}) collective-permute-start(bf16[448,768]{1,0:T(8,128)(2,1)} %add_convert_fusion.6), channel_id=1, source_target_pairs={{0,16},{4,20},{8,24},{12,28},{16,0},{20,4},{24,8},{28,12},{1,17},{... | collective-permute-start | bytes 2064392 | tf_op jit(solution)/shard_map/ppermute | solution.py:43
  359.3 31.3 %collective-permute-start.45 = (bf16[2,192,2304]{2,1,0:T(8,128)(2,1)S(1)}, bf16[2,192,2304]{2,1,0:T(8,128)(2,1)S(1)}, u32[]{:S(2)}, u32[]{:S(2)}) collective-permute-start(bf16[2,192,2304]{2,1,0:T(8,128)(2,1)S(1)} %maximum_select_fusion.8), channel_id=1, source_target_pairs={{0,1},{1,0},{2,3},{3,2},{4,5},{5,4},{6,7},{7,6},{8,9},{9,8},{10,11... | collective-permute-start | bytes 5308424 | tf_op jit(solution)/shard_map/ppermute | solution.py:43
  361.3 28.5 %collective-permute-start.44 = (bf16[448,768]{1,0:T(8,128)(2,1)S(1)}, bf16[448,768]{1,0:T(8,128)(2,1)S(1)}, u32[]{:S(2)}, u32[]{:S(2)}) collective-permute-start(bf16[448,768]{1,0:T(8,128)(2,1)S(1)} %add_convert_fusion.5), channel_id=1, source_target_pairs={{0,8},{4,12},{8,0},{12,4},{16,24},{20,28},{24,16},{28,20},{1,9},{5... | collective-permute-start | bytes 2064392 | tf_op jit(solution)/shard_map/ppermute | solution.py:43
  363.9 29.2 %collective-permute-start.40 = (bf16[3,64,512]{2,1,0:T(8,128)(2,1)S(1)}, bf16[3,64,512]{2,1,0:T(8,128)(2,1)S(1)}, u32[]{:S(2)}, u32[]{:S(2)}) collective-permute-start(bf16[3,64,512]{2,1,0:T(8,128)(2,1)S(1)} %get-tuple-element.211), channel_id=1, source_target_pairs={{0,16},{4,20},{8,24},{12,28},{16,0},{20,4},{24,8},{28,12},{1,17},{... | collective-permute-start | bytes 589832 | tf_op jit(solution)/shard_map/ppermute | solution.py:26
  391.4 31.1 %collective-permute-start.46 = (bf16[896,768]{1,0:T(8,128)(2,1)S(1)}, bf16[896,768]{1,0:T(8,128)(2,1)S(1)}, u32[]{:S(2)}, u32[]{:S(2)}) collective-permute-start(bf16[896,768]{1,0:T(8,128)(2,1)S(1)} %maximum_select_fusion.10), channel_id=1, source_target_pairs={{0,4},{4,0},{8,12},{12,8},{16,20},{20,16},{24,28},{28,24},{1,5},{5... | collective-permute-start | bytes 4128776 | tf_op jit(solution)/shard_map/ppermute | solution.py:43
  (70 other events, 646.7 us)
